TPU v7x, 512 devices: a whole 4x4x16 slice. The times are simulated.
512 devices in a mesh: wide: 32 (over x_lo, z), grp: 16 (over y, x_hi, core).
Axes of the slice: x: 4 (x_hi: 2, x_lo: 2; x = x_hi * 2 + x_lo), y: 4, z: 16, core: 2. Of those that a mesh axis runs over, the one named last changes fastest.
Arguments:
- log_hazards: float32 [25, 25], replicated, may hold values from -0.5 to 0.5
- bit_order: int32 [25], replicated, may hold values from 0 to 24, each once
- patients: int32 [256], replicated, may hold values from 0 to 33554431, as said below
- start_dist: float32 [33554432], P(('wide', 'grp')), may hold values from 0.25 to 4
- start_adjoint: float32 [33554432], P(('wide', 'grp')), may hold values from -6 to 6
Outputs:
- distribution: float32 [33554432], P(('wide', 'grp'))
- loglik: float32 [], replicated
- gradient: float32 [25, 25], replicated
- empty_state: float32 [], replicated
Inputs may be any that keep to these rules, and one draw needn't show every extreme that they name: `patients`: each value is a set of events, bit e set when event e is present; every draw has a patient with no event and one with all 25. `bit_order`: A permutation of the events.
All inputs are finite; a program needn't handle non-finite values.
Results may differ from a plain program's by a relative error of at most 0.0003.
Values sent between devices are 32-bit elements; how exact they have to be, the bound alone decides.
A program may use at most 64 MiB of HBM per device.

v0:
```python
import jax
import jax.numpy as jnp
import numpy as np
from jax import lax
from jax.sharding import PartitionSpec as P

highest = lax.Precision.HIGHEST


def partner_2(value, axis, distance):
    mask = 2**distance
    pairs = [(source, source ^ mask) for source in range(lax.axis_size(axis))]
    return lax.ppermute(value, axis, pairs)


def bit_table(number, columns):
    positions = jnp.arange(number, dtype=jnp.int32)
    shifts = jnp.arange(columns, dtype=jnp.int32)
    return (positions[:, None] >> shifts[None, :] & 1).astype(jnp.float32)


def index_bits(position, columns):
    shifts = jnp.arange(columns, dtype=jnp.int32)
    return (position >> shifts & 1).astype(jnp.float32)


def pick_columns(matrix, ranges):
    return jnp.concatenate(
        [matrix[:, begin_at : begin_at + length] for begin_at, length in ranges], axis=1
    )


def order_table(ranges, count_bits):
    listed = [begin_at + offset for begin_at, length in ranges for offset in range(length)]
    table = np.zeros((count_bits, count_bits), np.float32)
    table[np.arange(count_bits), np.array(listed, np.int64)] = 1.0
    return jnp.asarray(table)


def lane_tables(lane_bits_count, lane_count):
    source = jnp.arange(lane_count, dtype=jnp.int32)
    blocks = []
    for lane_bit in range(lane_bits_count):
        stride = 2**lane_bit
        lower_half = source >> lane_bit & 1 == 0
        blocks.append(
            ((source[None, :] == source[:, None] + stride) & lower_half[:, None]).astype(
                jnp.float32
            )
        )
    return jnp.concatenate(blocks, axis=0)


def rate_maker(coupling, diagonal, layout, row_bits, lane_bits):
    row_ranges, lane_ranges, device_ranges, device_values, block_begin, block_count = layout
    block_rows = coupling[block_begin : block_begin + block_count]
    offsets = diagonal[block_begin : block_begin + block_count] + jnp.dot(
        pick_columns(block_rows, device_ranges), device_values, precision=highest
    )
    by_row = jnp.dot(row_bits, pick_columns(block_rows, row_ranges).T, precision=highest)
    by_lane = jnp.dot(lane_bits, pick_columns(block_rows, lane_ranges).T, precision=highest)

    def rate_of(position):
        return jnp.exp(
            offsets[position] + by_row[:, position][:, None] + by_lane[:, position][None, :]
        )

    return rate_of


def row_split(values, row_bit):
    row_count, lane_count = values.shape
    return values.reshape(row_count >> row_bit + 1, 2, 2**row_bit, lane_count)


def join_rows(lower_half, upper_half):
    paired = jnp.stack([lower_half, upper_half], axis=1)
    return paired.reshape(-1, paired.shape[-1])


def local_push(values, rate_of, lane_part, row_start, block_count, lane_push):
    summed = jnp.zeros_like(values)
    if lane_part > 0:
        stacked = jnp.concatenate(
            [rate_of(position) * values for position in range(lane_part)], axis=1
        )
        summed = jnp.dot(stacked, lane_push, precision=highest)
    for position in range(lane_part, block_count):
        moving = row_split(rate_of(position) * values, row_start + position - lane_part)
        summed = summed + join_rows(jnp.zeros_like(moving[:, 0]), moving[:, 0])
    return summed


def local_pull(values, rate_of, lane_part, row_start, block_count, lane_pull):
    summed = jnp.zeros_like(values)
    lane_count = values.shape[1]
    if lane_part > 0:
        partners = jnp.dot(values, lane_pull, precision=highest)
        for position in range(lane_part):
            summed = (
                summed
                + rate_of(position)
                * partners[:, position * lane_count : (position + 1) * lane_count]
            )
    for position in range(lane_part, block_count):
        row_bit = row_start + position - lane_part
        others = row_split(values, row_bit)
        rates = row_split(rate_of(position), row_bit)
        summed = summed + join_rows(rates[:, 0] * others[:, 1], jnp.zeros_like(others[:, 1]))
    return summed


def local_gradient(
    forward, adjoint, rate_of, lane_part, row_start, block_count, lane_pull, lane_low
):
    contribs = []
    lane_count = forward.shape[1]
    if lane_part > 0:
        partners = jnp.dot(adjoint, lane_pull, precision=highest)
        for position in range(lane_part):
            partner = partners[:, position * lane_count : (position + 1) * lane_count]
            contribs.append(
                rate_of(position) * forward * (partner - adjoint) * lane_low[position][None, :]
            )
    for position in range(lane_part, block_count):
        row_bit = row_start + position - lane_part
        others = row_split(adjoint, row_bit)
        rates = row_split(rate_of(position), row_bit)
        forwards = row_split(forward, row_bit)
        lower_term = rates[:, 0] * forwards[:, 0] * (others[:, 1] - others[:, 0])
        contribs.append(join_rows(lower_term, jnp.zeros_like(lower_term)))
    return contribs


def feature_row(contrib, row_bits, lane_bits, device_values, to_global, own_bit):
    per_row = jnp.sum(contrib, axis=1)
    per_lane = jnp.sum(contrib, axis=0)
    whole = jnp.sum(per_row)
    listed = jnp.concatenate(
        [
            jnp.dot(per_row, row_bits, precision=highest),
            jnp.dot(per_lane, lane_bits, precision=highest),
            whole * device_values,
        ]
    )
    own_column = (jnp.arange(to_global.shape[0], dtype=jnp.int32) == own_bit).astype(jnp.float32)
    return jnp.dot(listed, to_global, precision=highest) + whole * own_column


def body(log_hazards, bit_order, patients, start_dist, start_adjoint):
    count_bits = log_hazards.shape[0]
    local_count = start_dist.shape[0]
    patient_count = patients.shape[0]
    wide_count = lax.axis_size("wide")
    grp_count = lax.axis_size("grp")
    wide_bits = wide_count.bit_length() - 1
    grp_bits = grp_count.bit_length() - 1
    local_bits = local_count.bit_length() - 1
    lane_bits_count = min(7, local_bits - wide_bits - grp_bits)
    lane_count = 2**lane_bits_count
    row_count = local_count // lane_count
    row_bits_count = local_bits - lane_bits_count
    wide_index = lax.axis_index("wide")
    grp_index = lax.axis_index("grp")
    wide_values = index_bits(wide_index, wide_bits)
    grp_values = index_bits(grp_index, grp_bits)
    device_values = jnp.concatenate([grp_values, wide_values])
    shifts = jnp.arange(count_bits, dtype=jnp.int32)
    onehot = (bit_order[:, None] == shifts[None, :]).astype(jnp.float32)
    by_bits = jnp.dot(onehot.T, jnp.dot(log_hazards, onehot, precision=highest), precision=highest)
    diagonal = jnp.diagonal(by_bits)
    coupling = by_bits * (1.0 - jnp.eye(count_bits, dtype=jnp.float32))
    row_bits = bit_table(row_count, row_bits_count)
    lane_bits = bit_table(lane_count, lane_bits_count)
    lane_push = lane_tables(lane_bits_count, lane_count)
    lane_pull = lane_push.T
    lane_low = 1.0 - lane_bits.T
    home_rows = [(lane_bits_count, row_bits_count)]
    lane_ranges = [(0, lane_bits_count)]
    home_devices = [(local_bits, grp_bits), (local_bits + grp_bits, wide_bits)]
    home_rate = rate_maker(
        coupling,
        diagonal,
        (home_rows, lane_ranges, home_devices, device_values, 0, count_bits),
        row_bits,
        lane_bits,
    )
    home_global = order_table(home_rows + lane_ranges + home_devices, count_bits)
    away_rows = [(lane_bits_count, row_bits_count - grp_bits), (local_bits, grp_bits)]
    away_devices = [(local_bits - grp_bits, grp_bits), (local_bits + grp_bits, wide_bits)]
    away_rate = rate_maker(
        coupling,
        diagonal,
        (away_rows, lane_ranges, away_devices, device_values, local_bits, grp_bits),
        row_bits,
        lane_bits,
    )
    away_global = order_table(away_rows + lane_ranges + away_devices, count_bits)
    row_start = row_bits_count - grp_bits

    def regroup(values):
        three_way = values.reshape(grp_count, -1, lane_count)
        arrived = lax.all_to_all(three_way, "grp", split_axis=0, concat_axis=0, tiled=True)
        return arrived.reshape(row_count, lane_count)

    def wide_swap(values, wide_bit):
        return partner_2(values, "wide", wide_bit)

    denominator = jnp.ones((row_count, lane_count), jnp.float32)
    for position in range(lane_bits_count):
        denominator = denominator + home_rate(position) * lane_low[position][None, :]
    for position in range(lane_bits_count, local_bits):
        rates = row_split(home_rate(position), position - lane_bits_count)
        denominator = denominator + join_rows(rates[:, 0], jnp.zeros_like(rates[:, 0]))
    for grp_bit in range(grp_bits):
        denominator = denominator + home_rate(local_bits + grp_bit) * (1.0 - grp_values[grp_bit])
    for wide_bit in range(wide_bits):
        denominator = denominator + home_rate(local_bits + grp_bits + wide_bit) * (
            1.0 - wide_values[wide_bit]
        )
    row_iota = lax.broadcasted_iota(jnp.int32, (row_count, lane_count), 0)
    lane_iota = lax.broadcasted_iota(jnp.int32, (row_count, lane_count), 1)
    first_device = (wide_index == 0) & (grp_index == 0)
    first_state = first_device & (row_iota == 0) & (lane_iota == 0)
    source = jnp.where(first_state, float(2**count_bits), 0.0).astype(jnp.float32)
    forward = start_dist.reshape(row_count, lane_count)
    summed = source + local_push(forward, home_rate, lane_bits_count, 0, local_bits, lane_push)
    away = regroup(forward)
    summed = summed + regroup(local_push(away, away_rate, 0, row_start, grp_bits, lane_push))
    for wide_bit in range(wide_bits):
        received = wide_swap(home_rate(local_bits + grp_bits + wide_bit) * forward, wide_bit)
        summed = summed + wide_values[wide_bit] * received
    forward = summed / denominator
    present = patients[:, None] >> shifts[None, :] & 1
    state_index = jnp.sum(present << bit_order[None, :], axis=1)
    device_number = wide_index * grp_count + grp_index
    on_device = state_index >> local_bits == device_number
    local_index = jnp.where(on_device, state_index & local_count - 1, local_count)
    counts = (
        jnp.zeros((local_count,), jnp.float32)
        .at[local_index]
        .add(1.0, mode="drop")
        .reshape(row_count, lane_count)
    )
    flattened = forward.reshape(-1)
    picked = flattened[jnp.where(on_device, local_index, 0)]
    log_sum = jnp.sum(jnp.where(on_device, jnp.log(picked), 0.0))
    log_first = jnp.where(first_device, jnp.log(flattened[0]), 0.0)
    weights = counts / (patient_count * forward)
    adjoint = start_adjoint.reshape(row_count, lane_count) * 2.0 ** (-(count_bits // 2))
    summed = weights + local_pull(adjoint, home_rate, lane_bits_count, 0, local_bits, lane_pull)
    away = regroup(adjoint)
    summed = summed + regroup(local_pull(away, away_rate, 0, row_start, grp_bits, lane_pull))
    for wide_bit in range(wide_bits):
        received = wide_swap(adjoint, wide_bit)
        summed = (
            summed
            + (1.0 - wide_values[wide_bit]) * home_rate(local_bits + grp_bits + wide_bit) * received
        )
    adjoint = summed / denominator
    grad_rows = []
    home_terms = local_gradient(
        forward, adjoint, home_rate, lane_bits_count, 0, local_bits, lane_pull, lane_low
    )
    for position in range(local_bits):
        grad_rows.append(
            feature_row(
                home_terms[position], row_bits, lane_bits, device_values, home_global, position
            )
        )
    three_way = (grp_count, -1, lane_count)
    arrived = (
        lax.all_to_all(forward.reshape(three_way), "grp", split_axis=0, concat_axis=0, tiled=True),
        lax.all_to_all(adjoint.reshape(three_way), "grp", split_axis=0, concat_axis=0, tiled=True),
    )
    away_forward = arrived[0].reshape(row_count, lane_count)
    away_adjoint = arrived[1].reshape(row_count, lane_count)
    away_terms = local_gradient(
        away_forward, away_adjoint, away_rate, 0, row_start, grp_bits, lane_pull, lane_low
    )
    for position in range(grp_bits):
        grad_rows.append(
            feature_row(
                away_terms[position],
                row_bits,
                lane_bits,
                device_values,
                away_global,
                local_bits + position,
            )
        )
    for wide_bit in range(wide_bits):
        global_bit = local_bits + grp_bits + wide_bit
        received = wide_swap(adjoint, wide_bit)
        contrib = (
            (1.0 - wide_values[wide_bit]) * home_rate(global_bit) * forward * (received - adjoint)
        )
        grad_rows.append(
            feature_row(contrib, row_bits, lane_bits, device_values, home_global, global_bit)
        )
    partial_grad = jnp.stack(grad_rows)
    grad_total, log_total, empty_state = lax.psum(
        (partial_grad, log_sum, log_first), ("wide", "grp")
    )
    gradient = jnp.dot(onehot, jnp.dot(grad_total, onehot.T, precision=highest), precision=highest)
    loglik = log_total / patient_count
    distribution = jnp.where(first_state, 0.0, forward)
    return (distribution.reshape(-1), loglik, gradient, empty_state)


def solution(mesh):
    return jax.shard_map(
        body,
        mesh=mesh,
        in_specs=(P(), P(), P(), P(("wide", "grp")), P(("wide", "grp"))),
        out_specs=(P(("wide", "grp")), P(), P(), P()),
        check_vma=False,
    )
```

profile of v0, /device:TPU:1, one launch (start us, length us, event | category | flops | bytes accessed | tf_op | source)
XLA Modules:
  0.0 466.9 jit_solution(10316019383893845244)
XLA Ops:
  7.5 6.0 %fusion.490 = (f32[512]{0:T(512)S(1)}, f32[512,1]{0,1:T(1,128)}, f32[512,1]{0,1:T(1,128)S(1)}, f32[512,1]{0,1:T(1,128)S(1)}, f32[512,1]{0,1:T(1,128)S(1)}, /*ind...) fusion(f32[]{:T(128)} %broadcast.1002, f32[512,25]{0,1:T(8,128)S(1)} %fusion.133, ...), kind=kLoop, calls=%fused_computation.907 | loop fusion | flops 4096 | bytes 34852 | tf_op jit(solution)/shard_map/add | solution.py:65
  20.2 6.1 %slice_add_fusion.3 = (f32[512,1]{0,1:T(1,128)}, f32[512,1]{0,1:T(1,128)}, f32[512,1]{0,1:T(1,128)}, f32[512,1]{0,1:T(1,128)}, f32[512,1]{0,1:T(1,128)S(1)}, /*i...) fusion(f32[512,25]{0,1:T(8,128)S(1)} %fusion.133, f32[]{:T(128)} %bitcast.119, ...), kind=kLoop, calls=%fused_computation.517 | loop fusion | flops 4608 | bytes 36900 | tf_op jit(solution)/shard_map/add | solution.py:65
  26.5 2.5 fusion.100
  29.1 4.4 collective-permute-start
  33.4 4.9 %collective-permute-start.1 = (f32[512,128]{1,0:T(8,128)}, f32[512,128]{1,0:T(8,128)}, u32[]{:S(2)}, u32[]{:S(2)}) collective-permute-start(f32[512,128]{1,0:T(8,128)} %get-tuple-element.143), channel_id=1, source_target_pairs={{0,32},{16,48},{32,0},{48,16},{64,96},{80,112},{96,64},{112,80},{1... | collective-permute-start | bytes 786440 | tf_op jit(solution)/shard_map/ppermute | solution.py:13
  38.3 8.8 %collective-permute-start.2 = (f32[512,128]{1,0:T(8,128)}, f32[512,128]{1,0:T(8,128)}, u32[]{:S(2)}, u32[]{:S(2)}) collective-permute-start(f32[512,128]{1,0:T(8,128)} %get-tuple-element.144), channel_id=1, source_target_pairs={{0,64},{16,80},{32,96},{48,112},{64,0},{80,16},{96,32},{112,48},{1... | collective-permute-start | bytes 786440 | tf_op jit(solution)/shard_map/ppermute | solution.py:13
  47.2 7.9 %collective-permute-start.3 = (f32[512,128]{1,0:T(8,128)}, f32[512,128]{1,0:T(8,128)}, u32[]{:S(2)}, u32[]{:S(2)}) collective-permute-start(f32[512,128]{1,0:T(8,128)} %get-tuple-element.145), channel_id=1, source_target_pairs={{0,128},{16,144},{32,160},{48,176},{64,192},{80,208},{96,224},{112... | collective-permute-start | bytes 786440 | tf_op jit(solution)/shard_map/ppermute | solution.py:13
  55.1 3.1 collective-permute-start.4
  59.1 8.7 %all-to-all-start.2 = ((f32[16,32,128]{2,1,0:T(8,128)}), f32[16,32,128]{2,1,0:T(8,128)S(1)}, u32[]{:S(2)}, u32[]{:S(2)}) async-start(f32[16,32,128]{2,1,0:T(8,128)} %bitcast.160), calls=%async_computation.2 | async-start | bytes 524288 | tf_op jit(solution)/shard_map/all_to_all | solution.py:203
  71.5 3.1 fusion.264
  77.0 6.2 %fusion.483 = (f32[512]{0:T(512)S(1)}, f32[512,1]{0,1:T(1,128)}, f32[512,1]{0,1:T(1,128)}, f32[512]{0:T(512)S(1)}, f32[512,1]{0,1:T(1,128)}, /*index=5*/f32[512]...) fusion(f32[]{:T(128)} %broadcast.1002, ...), kind=kLoop, calls=%fused_computation.900 | loop fusion | flops 4096 | bytes 47140 | tf_op jit(solution)/shard_map/add | solution.py:65
  96.2 1.8 slice_multiply_fusion.25
  98.0 1.8 slice_multiply_fusion.31
  99.8 1.7 slice_multiply_fusion.29
  101.5 1.7 slice_multiply_fusion.28
  103.2 1.7 slice_multiply_fusion.27
  105.0 1.7 slice_multiply_fusion.26
  106.6 1.7 slice_multiply_fusion.30
  108.9 1.7 slice_multiply_fusion.24
  110.6 7.2 %all-to-all-start = ((f32[16,32,128]{2,1,0:T(8,128)}), f32[16,32,128]{2,1,0:T(8,128)S(1)}, u32[]{:S(2)}, u32[]{:S(2)}) async-start(f32[16,32,128]{2,1,0:T(8,128)} %bitcast.66), calls=%async_computation | async-start | bytes 524288 | tf_op jit(solution)/shard_map/all_to_all | solution.py:203
  117.8 2.1 slice_multiply_fusion.32
  119.9 6.6 %all-to-all-done = f32[16,32,128]{2,1,0:T(8,128)S(1)} async-done(((f32[16,32,128]{2,1,0:T(8,128)}), f32[16,32,128]{2,1,0:T(8,128)S(1)}, u32[]{:S(2)}, u32[]{:S(2)}) %all-to-all-start) | async-done | bytes 262176 | tf_op jit(solution)/shard_map/all_to_all | solution.py:203
  130.1 4.8 %all-to-all-start.3 = ((f32[16,32,128]{2,1,0:T(8,128)}), f32[16,32,128]{2,1,0:T(8,128)}, u32[]{:S(2)}, u32[]{:S(2)}) async-start(f32[16,32,128]{2,1,0:T(8,128)} %fusion.91), calls=%async_computation.3 | async-start | bytes 524288 | tf_op jit(solution)/shard_map/all_to_all | solution.py:203
  138.7 2.6 collective-permute-start.5
  141.3 3.1 collective-permute-start.6
  144.4 5.2 %collective-permute-start.7 = (f32[512,128]{1,0:T(8,128)}, f32[512,128]{1,0:T(8,128)}, u32[]{:S(2)}, u32[]{:S(2)}) collective-permute-start(f32[512,128]{1,0:T(8,128)} %get-tuple-element.113), channel_id=1, source_target_pairs={{0,64},{16,80},{32,96},{48,112},{64,0},{80,16},{96,32},{112,48},{1... | collective-permute-start | bytes 786440 | tf_op jit(solution)/shard_map/ppermute | solution.py:13
  149.6 1.9 collective-permute-start.8
  151.6 1.9 collective-permute-start.9
  153.5 9.0 %all-to-all-start.1 = ((f32[16,32,128]{2,1,0:T(8,128)}), f32[16,32,128]{2,1,0:T(8,128)}, u32[]{:S(2)}, u32[]{:S(2)}) async-start(f32[16,32,128]{2,1,0:T(8,128)} %fusion.93), calls=%async_computation.1 | async-start | bytes 524288 | tf_op jit(solution)/shard_map/all_to_all | solution.py:203
  164.4 1.7 stack.270
  167.0 1.8 stack.248
  169.5 1.7 stack.251
  171.2 1.7 stack.273
  172.9 1.7 stack.252
  186.8 1.6 reshape.968
  189.0 1.4 reshape.967
  200.4 2.7 scatter_custom_fusion
  203.2 1.5 slice_bitcast_fusion.31
  204.8 10.6 %fusion.84 = (f32[512,128]{1,0:T(8,128)}, f32[512,128]{1,0:T(8,128)}) fusion(f32[512,128]{1,0:T(8,128)} %bitcast.870, f32[512,128]{1,0:T(8,128)} %bitcast.863, f32[512,128]{1,0:T(8,128)} %bitcast.862, f32[512,896]{1,0:T(8,128)S(1)} %fusion.414, f32[16,32,128]{2,1,0:T(8,128)} %all-to-all-done.3, f32[1,2,256,128]{3,2,1,0:T(8,128)} %stack.278, ...), kind=kOutput, calls=%fused_computation.214 | convolution fusion | flops 713555968 | bytes 12508344 | tf_op jit(solution)/shard_map/dot_general | solution.py:87
  215.5 3.2 collective-permute-start.11
  218.7 7.5 %collective-permute-start.12 = (f32[512,128]{1,0:T(8,128)}, f32[512,128]{1,0:T(8,128)}, u32[]{:S(2)}, u32[]{:S(2)}) collective-permute-start(f32[512,128]{1,0:T(8,128)} %get-tuple-element.284), channel_id=1, source_target_pairs={{0,64},{16,80},{32,96},{48,112},{64,0},{80,16},{96,32},{112,48},{1... | collective-permute-start | bytes 786440 | tf_op jit(solution)/shard_map/ppermute | solution.py:13
  226.3 8.8 %collective-permute-start.13 = (f32[512,128]{1,0:T(8,128)}, f32[512,128]{1,0:T(8,128)}, u32[]{:S(2)}, u32[]{:S(2)}) collective-permute-start(f32[512,128]{1,0:T(8,128)} %get-tuple-element.284), channel_id=1, source_target_pairs={{0,128},{16,144},{32,160},{48,176},{64,192},{80,208},{96,224},{112... | collective-permute-start | bytes 786440 | tf_op jit(solution)/shard_map/ppermute | solution.py:13
  235.1 2.2 collective-permute-start.14
  237.3 1.9 fusion.498
  239.2 2.8 collective-permute-start.10
  252.1 9.2 %all-to-all-start.4 = ((f32[16,32,128]{2,1,0:T(8,128)}), f32[16,32,128]{2,1,0:T(8,128)S(1)}, u32[]{:S(2)}, u32[]{:S(2)}) async-start(f32[16,32,128]{2,1,0:T(8,128)} %bitcast.293), calls=%async_computation.4 | async-start | bytes 524288 | tf_op jit(solution)/shard_map/all_to_all | solution.py:273
  261.4 2.4 fusion.54
  267.0 1.4 convolution_bitcast_fusion.54
  271.5 1.6 convolution_bitcast_fusion.16
  275.1 1.5 convolution_bitcast_fusion.17
  277.9 1.9 fusion.477
  283.1 1.8 fusion.141
  285.6 2.9 gather_fusion.1
  288.5 1.7 fusion.140
  290.2 7.2 %all-to-all-start.5 = ((f32[16,32,128]{2,1,0:T(8,128)}), f32[16,32,128]{2,1,0:T(8,128)S(1)}, u32[]{:S(2)}, u32[]{:S(2)}) async-start(f32[16,32,128]{2,1,0:T(8,128)} %bitcast.295), calls=%async_computation.5 | async-start | bytes 524288 | tf_op jit(solution)/shard_map/all_to_all | solution.py:274
  300.6 1.8 fusion.139
  302.4 3.7 all-to-all-done.5
  306.1 1.8 pad_reduce_fusion.2
  314.7 1.7 subtract_multiply_fusion
  319.8 1.5 fusion.62
  326.6 11.2 %broadcast_multiply_fusion.1 = (f32[9]{0:T(128)S(1)}, f32[9]{0:T(128)S(1)}, f32[9]{0:T(128)S(1)}, f32[9]{0:T(128)S(1)}, f32[9]{0:T(128)S(1)}, /*index=5*/f32[9]{...) fusion(f32[]{:T(128)} %get-tuple-element.5, ...), kind=kLoop, calls=%fused_computation.779 | loop fusion | flops 171 | bytes 756 | tf_op jit(solution)/shard_map/mul | solution.py:143
  352.8 4.5 broadcast_multiply_fusion.19
  363.3 1.8 fusion.52
  365.1 98.9 %all-reduce.39 = (f32[]{:T(128)}, f32[25,25]{1,0:T(8,128)S(1)}, f32[]{:T(128)}) all-reduce(f32[]{:T(128)} %select_reduce_fusion, f32[25,25]{1,0:T(8,128)S(1)} %stack.321, f32[]{:T(128)S(6)} %select_n.72), channel_id=1, replica_groups=mesh['wide'=32,'grp'=16] {'wide','grp'}, use_global_device_ids=true, to_apply=%region_2.3 | all-reduce | flops 627 | bytes 5016 | tf_op jit(solution)/shard_map/psum | solution.py:302
  (526 shorter events, 124.5 us)
Async XLA Ops:
  0.7 69.5 %copy-start.43 = (f32[5]{0:T(128)}, f32[5]{0:T(128)S(1)}, u32[]{:S(2)}) copy-start(f32[5]{0:T(128)S(1)} %and_convert_fusion) | copy-start | bytes 64
  1.4 68.9 %copy-start.46 = (f32[4]{0:T(128)}, f32[4]{0:T(128)S(1)}, u32[]{:S(2)}) copy-start(f32[4]{0:T(128)S(1)} %and_convert_fusion.1) | copy-start | bytes 52
  6.3 22.6 %copy-start.83 = (f32[128]{0:T(128)}, f32[128]{0:T(128)S(1)}, u32[]{:S(2)}) copy-start(f32[128]{0:T(128)S(1)} %get-tuple-element.195) | copy-start | bytes 1540
  6.3 22.6 %copy-start.84 = (f32[128]{0:T(128)}, f32[128]{0:T(128)S(1)}, u32[]{:S(2)}) copy-start(f32[128]{0:T(128)S(1)} %get-tuple-element.196) | copy-start | bytes 1540
  6.3 22.6 %copy-start.85 = (f32[128]{0:T(128)}, f32[128]{0:T(128)S(1)}, u32[]{:S(2)}) copy-start(f32[128]{0:T(128)S(1)} %get-tuple-element.197) | copy-start | bytes 1540
  7.0 22.0 %copy-start.90 = (f32[128]{0:T(128)}, f32[128]{0:T(128)S(1)}, u32[]{:S(2)}) copy-start(f32[128]{0:T(128)S(1)} %get-tuple-element.181) | copy-start | bytes 1540
  7.0 22.0 %copy-start.92 = (f32[128]{0:T(128)}, f32[128]{0:T(128)S(1)}, u32[]{:S(2)}) copy-start(f32[128]{0:T(128)S(1)} %get-tuple-element.182) | copy-start | bytes 1540
  7.0 22.0 %copy-start.94 = (f32[128]{0:T(128)}, f32[128]{0:T(128)S(1)}, u32[]{:S(2)}) copy-start(f32[128]{0:T(128)S(1)} %get-tuple-element.183) | copy-start | bytes 1540
  7.0 22.0 %copy-start.96 = (f32[128]{0:T(128)}, f32[128]{0:T(128)S(1)}, u32[]{:S(2)}) copy-start(f32[128]{0:T(128)S(1)} %get-tuple-element.194) | copy-start | bytes 1540
  16.9 41.4 %copy-start.2 = (f32[65536]{0:T(1024)S(1)}, f32[65536]{0:T(1024)}, u32[]{:S(2)}) copy-start(f32[65536]{0:T(1024)} %param.11) | copy-start | bytes 786436
  26.4 57.0 %copy-start.62 = (f32[512,1]{0,1:T(1,128)}, f32[512,1]{0,1:T(1,128)S(1)}, u32[]{:S(2)}) copy-start(f32[512,1]{0,1:T(1,128)S(1)} %get-tuple-element.155) | copy-start | bytes 6148
  26.4 57.0 %copy-start.64 = (f32[512,1]{0,1:T(1,128)}, f32[512,1]{0,1:T(1,128)S(1)}, u32[]{:S(2)}) copy-start(f32[512,1]{0,1:T(1,128)S(1)} %get-tuple-element.151) | copy-start | bytes 6148
  26.4 57.0 %copy-start.66 = (f32[512,1]{0,1:T(1,128)}, f32[512,1]{0,1:T(1,128)S(1)}, u32[]{:S(2)}) copy-start(f32[512,1]{0,1:T(1,128)S(1)} %get-tuple-element.152) | copy-start | bytes 6148
  26.4 57.0 %copy-start.68 = (f32[512,1]{0,1:T(1,128)}, f32[512,1]{0,1:T(1,128)S(1)}, u32[]{:S(2)}) copy-start(f32[512,1]{0,1:T(1,128)S(1)} %get-tuple-element.153) | copy-start | bytes 6148
  26.4 57.0 %copy-start.70 = (f32[512,1]{0,1:T(1,128)}, f32[512,1]{0,1:T(1,128)S(1)}, u32[]{:S(2)}) copy-start(f32[512,1]{0,1:T(1,128)S(1)} %get-tuple-element.154) | copy-start | bytes 6148
  26.4 60.7 %copy-start.115 = (s32[256]{0:T(256)S(1)}, s32[256]{0:T(256)}, u32[]{:S(2)}) copy-start(s32[256]{0:T(256)} %param.9) | copy-start | bytes 3076
  26.4 60.7 %copy-start.116 = (s32[25]{0:T(128)S(1)}, s32[25]{0:T(128)}, u32[]{:S(2)}) copy-start(s32[25]{0:T(128)} %param.8) | copy-start | bytes 304
  29.0 59.5 %copy-start.40 = (f32[512,896]{1,0:T(8,128)}, f32[512,896]{1,0:T(8,128)S(1)}, u32[]{:S(2)}) copy-start(f32[512,896]{1,0:T(8,128)S(1)} %get-tuple-element.141) | copy-start | bytes 5505028
  29.1 109.6 %collective-permute-start = (f32[512,128]{1,0:T(8,128)}, f32[512,128]{1,0:T(8,128)}, u32[]{:S(2)}, u32[]{:S(2)}) collective-permute-start(f32[512,128]{1,0:T(8,128)} %get-tuple-element.142), channel_id=1, source_target_pairs={{0,16},{16,0},{32,48},{48,32},{64,80},{80,64},{96,112},{112,96},{1... | collective-permute-start | bytes 786440 | tf_op jit(solution)/shard_map/ppermute | solution.py:13
  33.4 107.9 %collective-permute-start.1 = (f32[512,128]{1,0:T(8,128)}, f32[512,128]{1,0:T(8,128)}, u32[]{:S(2)}, u32[]{:S(2)}) collective-permute-start(f32[512,128]{1,0:T(8,128)} %get-tuple-element.143), channel_id=1, source_target_pairs={{0,32},{16,48},{32,0},{48,16},{64,96},{80,112},{96,64},{112,80},{1... | collective-permute-start | bytes 786440 | tf_op jit(solution)/shard_map/ppermute | solution.py:13
  38.3 106.1 %collective-permute-start.2 = (f32[512,128]{1,0:T(8,128)}, f32[512,128]{1,0:T(8,128)}, u32[]{:S(2)}, u32[]{:S(2)}) collective-permute-start(f32[512,128]{1,0:T(8,128)} %get-tuple-element.144), channel_id=1, source_target_pairs={{0,64},{16,80},{32,96},{48,112},{64,0},{80,16},{96,32},{112,48},{1... | collective-permute-start | bytes 786440 | tf_op jit(solution)/shard_map/ppermute | solution.py:13
  47.2 102.5 %collective-permute-start.3 = (f32[512,128]{1,0:T(8,128)}, f32[512,128]{1,0:T(8,128)}, u32[]{:S(2)}, u32[]{:S(2)}) collective-permute-start(f32[512,128]{1,0:T(8,128)} %get-tuple-element.145), channel_id=1, source_target_pairs={{0,128},{16,144},{32,160},{48,176},{64,192},{80,208},{96,224},{112... | collective-permute-start | bytes 786440 | tf_op jit(solution)/shard_map/ppermute | solution.py:13
  55.1 96.5 %collective-permute-start.4 = (f32[512,128]{1,0:T(8,128)}, f32[512,128]{1,0:T(8,128)}, u32[]{:S(2)}, u32[]{:S(2)}) collective-permute-start(f32[512,128]{1,0:T(8,128)} %get-tuple-element.146), channel_id=1, source_target_pairs={{0,256},{16,272},{32,288},{48,304},{64,320},{80,336},{96,352},{112... | collective-permute-start | bytes 786440 | tf_op jit(solution)/shard_map/ppermute | solution.py:13
  59.1 51.5 %all-to-all-start.2 = ((f32[16,32,128]{2,1,0:T(8,128)}), f32[16,32,128]{2,1,0:T(8,128)S(1)}, u32[]{:S(2)}, u32[]{:S(2)}) async-start(f32[16,32,128]{2,1,0:T(8,128)} %bitcast.160), calls=%async_computation.2 | async-start | bytes 524288 | tf_op jit(solution)/shard_map/all_to_all | solution.py:203
  110.6 15.9 %all-to-all-start = ((f32[16,32,128]{2,1,0:T(8,128)}), f32[16,32,128]{2,1,0:T(8,128)S(1)}, u32[]{:S(2)}, u32[]{:S(2)}) async-start(f32[16,32,128]{2,1,0:T(8,128)} %bitcast.66), calls=%async_computation | async-start | bytes 524288 | tf_op jit(solution)/shard_map/all_to_all | solution.py:203
  130.1 23.4 %all-to-all-start.3 = ((f32[16,32,128]{2,1,0:T(8,128)}), f32[16,32,128]{2,1,0:T(8,128)}, u32[]{:S(2)}, u32[]{:S(2)}) async-start(f32[16,32,128]{2,1,0:T(8,128)} %fusion.91), calls=%async_computation.3 | async-start | bytes 524288 | tf_op jit(solution)/shard_map/all_to_all | solution.py:203
  135.0 28.0 %copy-start.32 = (f32[2,1,128,128]{3,2,1,0:T(8,128)S(1)}, f32[2,1,128,128]{3,2,1,0:T(8,128)}, u32[]{:S(2)}) copy-start(f32[2,1,128,128]{3,2,1,0:T(8,128)} %get-tuple-element.124) | copy-start | bytes 393220
  135.0 28.7 %copy-start.31 = (f32[2,1,128,128]{3,2,1,0:T(8,128)S(1)}, f32[2,1,128,128]{3,2,1,0:T(8,128)}, u32[]{:S(2)}) copy-start(f32[2,1,128,128]{3,2,1,0:T(8,128)} %get-tuple-element.123) | copy-start | bytes 393220
  136.9 29.3 %copy-start.30 = (f32[128,1,2,128]{3,2,1,0:T(2,128)S(1)}, f32[128,1,2,128]{3,2,1,0:T(2,128)}, u32[]{:S(2)}) copy-start(f32[128,1,2,128]{3,2,1,0:T(2,128)} %get-tuple-element.137) | copy-start | bytes 393220
  137.9 30.8 %copy-start.29 = (f32[128,1,2,128]{3,2,1,0:T(2,128)S(1)}, f32[128,1,2,128]{3,2,1,0:T(2,128)}, u32[]{:S(2)}) copy-start(f32[128,1,2,128]{3,2,1,0:T(2,128)} %get-tuple-element.138) | copy-start | bytes 393220
  138.7 66.0 %collective-permute-start.5 = (f32[512,128]{1,0:T(8,128)}, f32[512,128]{1,0:T(8,128)}, u32[]{:S(2)}, u32[]{:S(2)}) collective-permute-start(f32[512,128]{1,0:T(8,128)} %get-tuple-element.113), channel_id=1, source_target_pairs={{0,16},{16,0},{32,48},{48,32},{64,80},{80,64},{96,112},{112,96},{1... | collective-permute-start | bytes 786440 | tf_op jit(solution)/shard_map/ppermute | solution.py:13
  141.3 63.4 %collective-permute-start.6 = (f32[512,128]{1,0:T(8,128)}, f32[512,128]{1,0:T(8,128)}, u32[]{:S(2)}, u32[]{:S(2)}) collective-permute-start(f32[512,128]{1,0:T(8,128)} %get-tuple-element.113), channel_id=1, source_target_pairs={{0,32},{16,48},{32,0},{48,16},{64,96},{80,112},{96,64},{112,80},{1... | collective-permute-start | bytes 786440 | tf_op jit(solution)/shard_map/ppermute | solution.py:13
  144.4 60.3 %collective-permute-start.7 = (f32[512,128]{1,0:T(8,128)}, f32[512,128]{1,0:T(8,128)}, u32[]{:S(2)}, u32[]{:S(2)}) collective-permute-start(f32[512,128]{1,0:T(8,128)} %get-tuple-element.113), channel_id=1, source_target_pairs={{0,64},{16,80},{32,96},{48,112},{64,0},{80,16},{96,32},{112,48},{1... | collective-permute-start | bytes 786440 | tf_op jit(solution)/shard_map/ppermute | solution.py:13
  149.6 55.1 %collective-permute-start.8 = (f32[512,128]{1,0:T(8,128)}, f32[512,128]{1,0:T(8,128)}, u32[]{:S(2)}, u32[]{:S(2)}) collective-permute-start(f32[512,128]{1,0:T(8,128)} %get-tuple-element.113), channel_id=1, source_target_pairs={{0,128},{16,144},{32,160},{48,176},{64,192},{80,208},{96,224},{112... | collective-permute-start | bytes 786440 | tf_op jit(solution)/shard_map/ppermute | solution.py:13
  151.6 53.2 %collective-permute-start.9 = (f32[512,128]{1,0:T(8,128)}, f32[512,128]{1,0:T(8,128)}, u32[]{:S(2)}, u32[]{:S(2)}) collective-permute-start(f32[512,128]{1,0:T(8,128)} %get-tuple-element.113), channel_id=1, source_target_pairs={{0,256},{16,272},{32,288},{48,304},{64,320},{80,336},{96,352},{112... | collective-permute-start | bytes 786440 | tf_op jit(solution)/shard_map/ppermute | solution.py:13
  153.5 51.3 %all-to-all-start.1 = ((f32[16,32,128]{2,1,0:T(8,128)}), f32[16,32,128]{2,1,0:T(8,128)}, u32[]{:S(2)}, u32[]{:S(2)}) async-start(f32[16,32,128]{2,1,0:T(8,128)} %fusion.93), calls=%async_computation.1 | async-start | bytes 524288 | tf_op jit(solution)/shard_map/all_to_all | solution.py:203
  178.3 26.5 %copy-start.37 = (f32[8,2,32,128]{3,2,1,0:T(8,128)S(1)}, f32[8,2,32,128]{3,2,1,0:T(8,128)}, u32[]{:S(2)}) copy-start(f32[8,2,32,128]{3,2,1,0:T(8,128)} %stack.253) | copy-start | bytes 786436
  215.5 26.5 %copy-start.17 = (f32[256,2,1,128]{3,1,0,2:T(2,128)S(1)}, f32[256,2,1,128]{3,1,0,2:T(2,128)}, u32[]{:S(2)}) copy-start(f32[256,2,1,128]{3,1,0,2:T(2,128)} %add_exponential_fusion.17) | copy-start | bytes 786436
  215.5 28.9 %copy-start.16 = (f32[128,2,2,128]{3,2,1,0:T(2,128)S(1)}, f32[128,2,2,128]{3,2,1,0:T(2,128)}, u32[]{:S(2)}) copy-start(f32[128,2,2,128]{3,2,1,0:T(2,128)} %copy-done.15) | copy-start | bytes 786436
  215.5 99.1 %collective-permute-start.11 = (f32[512,128]{1,0:T(8,128)}, f32[512,128]{1,0:T(8,128)}, u32[]{:S(2)}, u32[]{:S(2)}) collective-permute-start(f32[512,128]{1,0:T(8,128)} %get-tuple-element.284), channel_id=1, source_target_pairs={{0,32},{16,48},{32,0},{48,16},{64,96},{80,112},{96,64},{112,80},{1... | collective-permute-start | bytes 786440 | tf_op jit(solution)/shard_map/ppermute | solution.py:13
  218.7 95.8 %collective-permute-start.12 = (f32[512,128]{1,0:T(8,128)}, f32[512,128]{1,0:T(8,128)}, u32[]{:S(2)}, u32[]{:S(2)}) collective-permute-start(f32[512,128]{1,0:T(8,128)} %get-tuple-element.284), channel_id=1, source_target_pairs={{0,64},{16,80},{32,96},{48,112},{64,0},{80,16},{96,32},{112,48},{1... | collective-permute-start | bytes 786440 | tf_op jit(solution)/shard_map/ppermute | solution.py:13
  226.3 88.3 %collective-permute-start.13 = (f32[512,128]{1,0:T(8,128)}, f32[512,128]{1,0:T(8,128)}, u32[]{:S(2)}, u32[]{:S(2)}) collective-permute-start(f32[512,128]{1,0:T(8,128)} %get-tuple-element.284), channel_id=1, source_target_pairs={{0,128},{16,144},{32,160},{48,176},{64,192},{80,208},{96,224},{112... | collective-permute-start | bytes 786440 | tf_op jit(solution)/shard_map/ppermute | solution.py:13
  235.1 79.5 %collective-permute-start.14 = (f32[512,128]{1,0:T(8,128)}, f32[512,128]{1,0:T(8,128)}, u32[]{:S(2)}, u32[]{:S(2)}) collective-permute-start(f32[512,128]{1,0:T(8,128)} %get-tuple-element.284), channel_id=1, source_target_pairs={{0,256},{16,272},{32,288},{48,304},{64,320},{80,336},{96,352},{112... | collective-permute-start | bytes 786440 | tf_op jit(solution)/shard_map/ppermute | solution.py:13
  239.2 80.5 %collective-permute-start.10 = (f32[512,128]{1,0:T(8,128)}, f32[512,128]{1,0:T(8,128)}, u32[]{:S(2)}, u32[]{:S(2)}) collective-permute-start(f32[512,128]{1,0:T(8,128)} %get-tuple-element.284), channel_id=1, source_target_pairs={{0,16},{16,0},{32,48},{48,32},{64,80},{80,64},{96,112},{112,96},{1... | collective-permute-start | bytes 786440 | tf_op jit(solution)/shard_map/ppermute | solution.py:13
  252.1 38.1 %all-to-all-start.4 = ((f32[16,32,128]{2,1,0:T(8,128)}), f32[16,32,128]{2,1,0:T(8,128)S(1)}, u32[]{:S(2)}, u32[]{:S(2)}) async-start(f32[16,32,128]{2,1,0:T(8,128)} %bitcast.293), calls=%async_computation.4 | async-start | bytes 524288 | tf_op jit(solution)/shard_map/all_to_all | solution.py:273
  283.1 23.1 %copy-start.4 = (f32[1,2,256,128]{3,2,1,0:T(8,128)S(1)}, f32[1,2,256,128]{3,2,1,0:T(8,128)}, u32[]{:S(2)}) copy-start(f32[1,2,256,128]{3,2,1,0:T(8,128)} %add_exponential_fusion.5) | copy-start | bytes 786436
  290.2 15.9 %all-to-all-start.5 = ((f32[16,32,128]{2,1,0:T(8,128)}), f32[16,32,128]{2,1,0:T(8,128)S(1)}, u32[]{:S(2)}, u32[]{:S(2)}) async-start(f32[16,32,128]{2,1,0:T(8,128)} %bitcast.295), calls=%async_computation.5 | async-start | bytes 524288 | tf_op jit(solution)/shard_map/all_to_all | solution.py:274
  321.3 27.2 %copy-start.122 = (f32[9]{0:T(128)S(1)}, f32[9]{0:T(128)}, u32[]{:S(2)}) copy-start(f32[9]{0:T(128)} %convolution_bitcast_fusion.13) | copy-start | bytes 112
  321.4 27.2 %copy-start.123 = (f32[7]{0:T(128)S(1)}, f32[7]{0:T(128)}, u32[]{:S(2)}) copy-start(f32[7]{0:T(128)} %convolution_bitcast_fusion.52) | copy-start | bytes 88
  321.4 28.0 %copy-start.124 = (f32[9]{0:T(128)S(1)}, f32[9]{0:T(128)}, u32[]{:S(2)}) copy-start(f32[9]{0:T(128)} %convolution_bitcast_fusion.14) | copy-start | bytes 112
  321.4 28.0 %copy-start.125 = (f32[7]{0:T(128)S(1)}, f32[7]{0:T(128)}, u32[]{:S(2)}) copy-start(f32[7]{0:T(128)} %convolution_bitcast_fusion.54) | copy-start | bytes 88
  321.4 28.8 %copy-start.126 = (f32[9]{0:T(128)S(1)}, f32[9]{0:T(128)}, u32[]{:S(2)}) copy-start(f32[9]{0:T(128)} %convolution_bitcast_fusion.15) | copy-start | bytes 112
  321.4 28.8 %copy-start.127 = (f32[7]{0:T(128)S(1)}, f32[7]{0:T(128)}, u32[]{:S(2)}) copy-start(f32[7]{0:T(128)} %convolution_bitcast_fusion.56) | copy-start | bytes 88
  321.4 29.6 %copy-start.128 = (f32[9]{0:T(128)S(1)}, f32[9]{0:T(128)}, u32[]{:S(2)}) copy-start(f32[9]{0:T(128)} %convolution_bitcast_fusion.16) | copy-start | bytes 112
  321.4 29.6 %copy-start.130 = (f32[7]{0:T(128)S(1)}, f32[7]{0:T(128)}, u32[]{:S(2)}) copy-start(f32[7]{0:T(128)} %convolution_bitcast_fusion.58) | copy-start | bytes 88
  321.4 30.5 %copy-start.129 = (f32[9]{0:T(128)S(1)}, f32[9]{0:T(128)}, u32[]{:S(2)}) copy-start(f32[9]{0:T(128)} %convolution_bitcast_fusion.17) | copy-start | bytes 112
  321.4 30.5 %copy-start.131 = (f32[7]{0:T(128)S(1)}, f32[7]{0:T(128)}, u32[]{:S(2)}) copy-start(f32[7]{0:T(128)} %convolution_bitcast_fusion.60) | copy-start | bytes 88
  321.4 36.7 %copy-start.119 = (f32[9]{0:T(128)S(1)}, f32[9]{0:T(128)}, u32[]{:S(2)}) copy-start(f32[9]{0:T(128)} %convolution_bitcast_fusion.19) | copy-start | bytes 112
  321.5 36.7 %copy-start.120 = (f32[7]{0:T(128)S(1)}, f32[7]{0:T(128)}, u32[]{:S(2)}) copy-start(f32[7]{0:T(128)} %convolution_bitcast_fusion.64) | copy-start | bytes 88
  321.5 37.5 %copy-start.118 = (f32[9]{0:T(128)S(1)}, f32[9]{0:T(128)}, u32[]{:S(2)}) copy-start(f32[9]{0:T(128)} %convolution_bitcast_fusion.20) | copy-start | bytes 112
  321.5 37.5 %copy-start.121 = (f32[7]{0:T(128)S(1)}, f32[7]{0:T(128)}, u32[]{:S(2)}) copy-start(f32[7]{0:T(128)} %convolution_bitcast_fusion.66) | copy-start | bytes 88
  321.5 41.8 %copy-start.132 = (pred[128]{0:T(512)(128)(4,1)S(1)}, pred[128]{0:T(512)(128)(4,1)}, u32[]{:S(2)}) copy-start(pred[128]{0:T(512)(128)(4,1)} %iota_compare_fusion.12) | copy-start | bytes 388
  321.5 41.8 %copy-start.133 = (pred[512]{0:T(512)(128)(4,1)S(1)}, pred[512]{0:T(512)(128)(4,1)}, u32[]{:S(2)}) copy-start(pred[512]{0:T(512)(128)(4,1)} %fusion.269) | copy-start | bytes 1540
  321.5 142.6 %copy-start.117 = (s32[25]{0:T(128)S(1)}, s32[25]{0:T(128)}, u32[]{:S(2)}) copy-start(s32[25]{0:T(128)} %param.8) | copy-start | bytes 304
  (91 other events, 799.5 us)
where the time goes:
time: 470 us; the launch traced here: 467 us
  starting transfers between devices  115 us (24%)
  other arithmetic  114 us (24%)
  blocking collectives  98.9 us (21%)
  matrix products  61.7 us (13%)
  local copies, waits for them, and re-layouts  56.2 us (12%)
  between operations  11 us (2%)
  waiting for transfers between devices  10.4 us (2%)
    psum x1, blocking collectives, body(): lax.psum((partial_grad, log_sum, log_first), ('wide', 'grp'))  98.9 us
    ppermute x15, starting transfers between devices, partner_2(): return lax.ppermute(value, axis, pairs)  68.5 us
    all_to_all x4, starting transfers between devices, regroup(): lax.all_to_all(three_way, 'grp', split_axis=0, concat_axis=0, tiled=True)  29.7 us
    add x4, other arithmetic, rate_of(): offsets[position] + by_row[:, position][:, None]  21.3 us
    dot_general x25, matrix products, feature_row(): return jnp.dot(listed, to_global, precision=highest) + whole * own_column  20.8 us
    another operation x26, local copies, waits for them, and re-layouts, join_rows(): paired = jnp.stack([lower_half, upper_half], axis=1)  20.4 us
    mul x13, other arithmetic, local_pull(): rates[:, 0] * others[:, 1]  18.7 us
    mul x2, other arithmetic, feature_row(): whole * device_values  15.8 us
  transfers between devices with their start and end apart: 21, of which 2 were waited for; matrix products, arithmetic and copies ran while one was open for 31% of the time, Pallas kernels for 0%

commit v1 on v0

v1 whole, which is shorter than its diff:
```python
import jax
import jax.numpy as jnp
from jax import lax
from jax.experimental import pallas as pl
from jax.experimental.pallas import tpu as pltpu
from jax.sharding import PartitionSpec as P

MESH = pl.DeviceIdType.MESH
HIGH = lax.Precision.HIGHEST
F32 = jnp.float32

EVENTS = 25
PATIENTS = 256
LANES = 128
ROWS = 512
HALF = 256
CHUNK = 128
CHUNKS = 4
PIECE = 64
PIECES = 4
HOPS = 8
FIRST_DEVICE_BIT = 16
Z_BITS = ((20, 1), (21, 2), (22, 4), (23, 8))
CROSS = ((16, "grp", 1), (17, "grp", 2), (18, "grp", 4), (19, "grp", 8), (24, "wide", 16))
STAGES = (
    (((1,), ()),),
    (((2,), ()), ((), (16,)), ((2,), (16,))),
    (((4,), ()), ((8,), ()), ((4, 8), ())),
    (((), (1,)), ((), (2,)), ((), (1, 2))),
    (((), (4,)), ((), (8,)), ((), (4, 8))),
)
COLUMNS = EVENTS + 2
UP_ORDER = (0, 2, 1, 3)
DOWN_ORDER = (0, 1, 2, 3)


def nn(left, right):
    return lax.dot_general(
        left, right, (((1,), (0,)), ((), ())), precision=HIGH, preferred_element_type=F32
    )


def nt(left, right):
    return lax.dot_general(
        left, right, (((1,), (1,)), ((), ())), precision=HIGH, preferred_element_type=F32
    )


def iota(shape, axis):
    return lax.broadcasted_iota(jnp.int32, shape, axis)


def flip(index, distances):
    for distance in distances:
        index = index + distance - 2 * distance * ((index // distance) % 2)
    return index


def kernel(
    hazards_ref,
    order_ref,
    patients_ref,
    p_ref,
    q_ref,
    dist_ref,
    grad_ref,
    loglik_ref,
    empty_ref,
    rate,
    inverse,
    sum_f,
    sum_a,
    fwd,
    adj,
    counts,
    folded,
    ring_p,
    ring_q,
    ring_f,
    ring_a,
    cross_in,
    cross_half,
    reduce_out,
    reduce_in,
    onehot,
    hazards,
    tables,
    p_send,
    p_recv,
    q_send,
    q_recv,
    f_send,
    f_recv,
    a_send,
    a_recv,
    x_send,
    x_recv,
    h_send,
    h_recv,
    r_send,
    r_recv,
):
    wide = lax.axis_index("wide")
    grp = lax.axis_index("grp")
    device = wide * 16 + grp
    place = wide % 16
    above = {"wide": wide - place + (place + 1) % 16}
    below = {"wide": wide - place + (place + 15) % 16}

    def device_bit(bit):
        return (device // 2 ** (bit - FIRST_DEVICE_BIT)) % 2

    def partner(axis, distance):
        return {axis: flip(grp if axis == "grp" else wide, (distance,))}

    def remote(source, target, send, receive, where):
        return pltpu.make_async_remote_copy(
            src_ref=source,
            dst_ref=target,
            send_sem=send,
            recv_sem=receive,
            device_id=where,
            device_id_type=MESH,
        )

    barrier = pltpu.get_barrier_semaphore()
    neighbours = [above, below] + [partner(axis, distance) for _, axis, distance in CROSS]
    for neighbour in neighbours:
        pl.semaphore_signal(barrier, inc=1, device_id=neighbour, device_id_type=MESH)
    pl.semaphore_wait(barrier, len(neighbours))

    started = []

    def rows_of(chunk):
        return pl.ds(chunk * CHUNK, CHUNK)

    def up_copy(hop, chunk):
        rows = rows_of(chunk)
        source = p_ref.at[rows] if hop == 1 else ring_p.at[hop - 2, rows]
        return remote(
            source, ring_p.at[hop - 1, rows], p_send.at[hop - 1, chunk], p_recv.at[hop - 1, chunk], above
        )

    def down_copy(hop, chunk):
        rows = rows_of(chunk)
        source = q_ref.at[rows] if hop == 1 else ring_q.at[hop - 2, rows]
        return remote(
            source, ring_q.at[hop - 1, rows], q_send.at[hop - 1, chunk], q_recv.at[hop - 1, chunk], below
        )

    def up_half(hop, piece):
        rows = pl.ds(piece * PIECE, PIECE)
        if hop == 1:
            source = fwd.at[pl.ds(HALF + piece * PIECE, PIECE)]
        else:
            source = ring_f.at[hop - 2, rows]
        return remote(
            source, ring_f.at[hop - 1, rows], f_send.at[hop - 1, piece], f_recv.at[hop - 1, piece], above
        )

    def down_half(hop, piece):
        rows = pl.ds(piece * PIECE, PIECE)
        source = adj.at[rows] if hop == 1 else ring_a.at[hop - 2, rows]
        return remote(
            source, ring_a.at[hop - 1, rows], a_send.at[hop - 1, piece], a_recv.at[hop - 1, piece], below
        )

    def begin(copy):
        copy.start()
        started.append(copy)

    for up, down in zip(UP_ORDER, DOWN_ORDER):
        begin(up_copy(1, up))
        begin(down_copy(1, down))

    def cross_copy(number, source, target, send, receive):
        _, axis, distance = CROSS[number]
        return remote(
            source, target.at[number], send.at[number], receive.at[number], partner(axis, distance)
        )

    def cross_start(low, high, target, send, receive):
        for number, (bit, _, _) in enumerate(CROSS):
            for value, source in ((0, low), (1, high)):

                @pl.when(device_bit(bit) == value)
                def _():
                    cross_copy(number, source, target, send, receive).start()

            started.append(cross_copy(number, low, target, send, receive))

    cross_start(p_ref, q_ref, cross_in, x_send, x_recv)

    lane_id = iota((1, LANES), 1)
    lane_has = [((lane_id >> bit) & 1).astype(F32) for bit in range(7)]
    sub_id = iota((1, 8, LANES), 1)
    sub_has = [((sub_id >> bit) & 1).astype(F32) for bit in range(3)]

    def make_tables():
        lane8 = iota((8, LANES), 1)
        sub8 = iota((8, LANES), 0)
        hazards[...] = jnp.zeros_like(hazards)
        hazards[0:EVENTS, 0:EVENTS] = hazards_ref[...]
        onehot[...] = jnp.zeros_like(onehot)
        for tile in range(4):
            block = jnp.zeros((8, LANES), F32)
            for event in range(8 * tile, min(8 * tile + 8, EVENTS)):
                hit = (sub8 == event - 8 * tile) & (lane8 == order_ref[event])
                block = jnp.where(hit, 1.0, block)
            onehot[8 * tile : 8 * tile + 8, :] = block
        by_event = onehot[...]
        by_bit = by_event.T
        matrix = nn(by_bit, nn(hazards[...], by_event))
        square = (LANES, LANES)
        sub = iota(square, 0)
        lane = iota(square, 1)
        same = sub == lane
        diagonal = jnp.sum(jnp.where(same, matrix, 0.0), axis=1, keepdims=True)
        coupling = jnp.where(same, 0.0, matrix)
        lane_bits = jnp.where(sub < 7, (lane >> jnp.minimum(sub, 7)) & 1, 0).astype(F32)
        tables[ROWS : ROWS + 32, :] = jnp.exp(nn(coupling[0:32], lane_bits))
        row = iota((ROWS, LANES), 0)
        column = iota((ROWS, LANES), 1)
        row_bit = (row >> jnp.clip(column - 7, 0, 8)) & 1
        dev_bit = (device >> jnp.clip(column - FIRST_DEVICE_BIT, 0, 8)) & 1
        bits = jnp.where(column < 7, 0, jnp.where(column < 16, row_bit, dev_bit))
        features = jnp.where(column < EVENTS, bits, jnp.where(column == EVENTS, 1, 0)).astype(F32)
        widened = jnp.where(lane == EVENTS, diagonal, coupling)
        tables[0:ROWS, :] = jnp.exp(nt(features, widened))

    def make_rate(bit):
        def run():
            row_factor = tables[0:ROWS, bit : bit + 1]
            lane_factor = tables[ROWS + bit : ROWS + bit + 1, :]
            rate[bit] = row_factor * lane_factor

        return run

    def chunk_groups(values):
        return values.reshape(CHUNK // 8, 8, LANES)

    def lower_rows(values, distance):
        split = values.reshape(CHUNK // (2 * distance), 2, distance, LANES)
        low = split[:, 0:1]
        return jnp.concatenate([low, jnp.zeros_like(low)], axis=1).reshape(CHUNK, LANES)

    def make_inverse(chunk):
        def run():
            rows = rows_of(chunk)
            total = jnp.ones((CHUNK, LANES), F32)
            for bit in range(7):
                total = total + rate[bit, rows] * (1.0 - lane_has[bit])
            for bit in range(3):
                part = chunk_groups(rate[7 + bit, rows]) * (1.0 - sub_has[bit])
                total = total + part.reshape(CHUNK, LANES)
            for bit in range(4):
                total = total + lower_rows(rate[10 + bit, rows], 8 * 2**bit)
            if chunk % 2 == 0:
                total = total + rate[14, rows]
            if chunk < 2:
                total = total + rate[15, rows]
            for bit in range(FIRST_DEVICE_BIT, EVENTS):
                total = total + rate[bit, rows] * (1 - device_bit(bit)).astype(F32)
            inverse[rows] = 1.0 / total

        return run

    def local_forward(chunk):
        def run():
            rows = rows_of(chunk)
            values = p_ref[rows]
            total = jnp.zeros((CHUNK, LANES), F32)
            for bit in range(7):
                total = total + pltpu.roll(rate[bit, rows] * values, 2**bit, 1) * lane_has[bit]
            for bit in range(3):
                moved = pltpu.roll(chunk_groups(rate[7 + bit, rows] * values), 2**bit, 1)
                total = total + (moved * sub_has[bit]).reshape(CHUNK, LANES)
            for bit in range(4):
                distance = 8 * 2**bit
                split = (rate[10 + bit, rows] * values).reshape(
                    CHUNK // (2 * distance), 2, distance, LANES
                )
                low = split[:, 0:1]
                total = total + jnp.concatenate([jnp.zeros_like(low), low], axis=1).reshape(
                    CHUNK, LANES
                )
            if chunk % 2 == 1:
                other = rows_of(chunk - 1)
                total = total + rate[14, other] * p_ref[other]
            if chunk >= 2:
                other = rows_of(chunk - 2)
                total = total + rate[15, other] * p_ref[other]
            sum_f[rows] = total

        return run

    def local_adjoint(chunk):
        def run():
            rows = rows_of(chunk)
            values = q_ref[rows]
            total = jnp.zeros((CHUNK, LANES), F32)
            for bit in range(7):
                moved = pltpu.roll(values, LANES - 2**bit, 1)
                total = total + rate[bit, rows] * moved * (1.0 - lane_has[bit])
            grouped = chunk_groups(values)
            for bit in range(3):
                moved = pltpu.roll(grouped, 8 - 2**bit, 1) * (1.0 - sub_has[bit])
                total = total + rate[7 + bit, rows] * moved.reshape(CHUNK, LANES)
            for bit in range(4):
                distance = 8 * 2**bit
                split = values.reshape(CHUNK // (2 * distance), 2, distance, LANES)
                rates = rate[10 + bit, rows].reshape(split.shape)
                low = rates[:, 0:1] * split[:, 1:2]
                total = total + jnp.concatenate([low, jnp.zeros_like(low)], axis=1).reshape(
                    CHUNK, LANES
                )
            if chunk % 2 == 0:
                total = total + rate[14, rows] * q_ref[rows_of(chunk + 1)]
            if chunk < 2:
                total = total + rate[15, rows] * q_ref[rows_of(chunk + 2)]
            sum_a[rows] = total

        return run

    def make_counts():
        total = jnp.zeros((ROWS, LANES), F32)
        for part in range(PATIENTS // LANES):
            people = patients_ref[part : part + 1, :]
            state = jnp.zeros((1, LANES), jnp.int32)
            for event in range(EVENTS):
                state = state + (((people >> event) & 1) << order_ref[event])
            here = (state >> 16) == device
            row = jnp.where(here, (state >> 7) & (ROWS - 1), -1)
            lane = state & (LANES - 1)
            in_row = jnp.where(iota((ROWS, LANES), 0) == row, 1.0, 0.0)
            in_lane = jnp.where(iota((LANES, LANES), 0) == lane, 1.0, 0.0)
            total = total + lax.dot_general(
                in_row.astype(jnp.bfloat16),
                in_lane.astype(jnp.bfloat16),
                (((1,), (1,)), ((), ())),
                preferred_element_type=F32,
            )
        counts[...] = total

    def add_pair(bit, up, down):
        has = device_bit(bit).astype(F32)
        sum_f[...] += rate[bit] * up[...] * has
        sum_a[...] += rate[bit] * down[...] * (1.0 - has)

    def add_cross(number):
        def run():
            bit = CROSS[number][0]
            cross_copy(number, p_ref, cross_in, x_send, x_recv).wait_recv()
            add_pair(bit, cross_in.at[number], cross_in.at[number])

        return run

    def add_ring(bit, hop):
        def run():
            add_pair(bit, ring_p.at[hop - 1], ring_q.at[hop - 1])

        return run

    tasks = [make_tables]
    tasks += [make_rate(bit) for bit in range(EVENTS)]
    tasks += [make_counts]
    for chunk in range(CHUNKS):
        tasks += [make_inverse(chunk), local_forward(chunk), local_adjoint(chunk)]
    tasks += [add_cross(number) for number in range(len(CROSS))]
    tasks += [add_ring(20, 1), add_ring(21, 2)]
    slots = (HOPS - 1) * CHUNKS
    late = {5 * CHUNKS: add_ring(22, 4)}
    done = 0
    for hop in range(1, HOPS):
        for step, (up, down) in enumerate(zip(UP_ORDER, DOWN_ORDER)):
            slot = (hop - 1) * CHUNKS + step
            goal = -(-len(tasks) * (slot + 1) // (slots - CHUNKS))
            while done < min(goal, len(tasks)):
                tasks[done]()
                done += 1
            if slot in late:
                late[slot]()
            up_copy(hop, up).wait_recv()
            begin(up_copy(hop + 1, up))
            down_copy(hop, down).wait_recv()
            begin(down_copy(hop + 1, down))

    first_device = device == 0

    def finish_forward(chunk):
        rows = rows_of(chunk)
        has = device_bit(23).astype(F32)
        total = sum_f[rows] + rate[23, rows] * ring_p[HOPS - 1, rows] * has
        if chunk == 0:
            spot = (iota((CHUNK, LANES), 0) == 0) & (iota((CHUNK, LANES), 1) == 0) & first_device
            total = total + jnp.where(spot, float(2**EVENTS), 0.0)
            values = total * inverse[rows]
            dist_ref[rows] = jnp.where(spot, 0.0, values)
        else:
            values = total * inverse[rows]
            dist_ref[rows] = values
        fwd[rows] = values

    def finish_adjoint(chunk):
        rows = rows_of(chunk)
        lacks = 1.0 - device_bit(23).astype(F32)
        total = sum_a[rows] + rate[23, rows] * ring_q[HOPS - 1, rows] * lacks
        weights = counts[rows] / (float(PATIENTS) * fwd[rows])
        adj[rows] = (weights + total * 2.0**-12) * inverse[rows]

    for step, (up, down) in enumerate(zip(UP_ORDER, DOWN_ORDER)):
        up_copy(HOPS, up).wait_recv()
        finish_forward(up)
        if up >= 2:
            for piece in (2 * up - 4, 2 * up - 3):
                begin(up_half(1, piece))
        down_copy(HOPS, down).wait_recv()
        ready = [c for c in DOWN_ORDER[: step + 1] if c in UP_ORDER[: step + 1]]
        before = [c for c in DOWN_ORDER[:step] if c in UP_ORDER[:step]]
        for chunk in ready:
            if chunk not in before:
                finish_adjoint(chunk)
                if chunk < 2:
                    for piece in (2 * chunk, 2 * chunk + 1):
                        begin(down_half(1, piece))

    upper = pl.ds(HALF, HALF)
    lower = pl.ds(0, HALF)
    cross_start(fwd.at[upper], adj.at[lower], cross_half, h_send, h_recv)

    def put(column, total, parts):
        at = pl.ds(column * LANES, LANES)
        folded[0:8, at] = total
        for bit in range(6):
            folded[8 * bit + 8 : 8 * bit + 16, at] = parts[bit]

    def fold(values, bits):
        zero = jnp.zeros((8, LANES), F32)
        parts = [zero] * 6
        rest = values
        for position in reversed(range(len(bits))):
            size = 2**position
            high = rest[size:]
            parts[bits[position]] = jnp.sum(high, axis=0)
            rest = rest[:size] + high
        return rest[0], parts

    every = (0, 1, 2, 3, 4, 5)

    def gradient_lane(bit):
        def run():
            values = adj[...]
            moved = pltpu.roll(values, LANES - 2**bit, 1)
            term = rate[bit] * fwd[...] * (moved - values) * (1.0 - lane_has[bit])
            put(bit, *fold(term.reshape(64, 8, LANES), every))

        return run

    def gradient_sub(bit):
        def run():
            values = adj[...].reshape(64, 8, LANES)
            moved = pltpu.roll(values, 8 - 2**bit, 1)
            scaled = (rate[7 + bit] * fwd[...]).reshape(64, 8, LANES)
            term = scaled * (moved - values) * (1.0 - sub_has[bit])
            put(7 + bit, *fold(term, every))

        return run

    def gradient_row(bit):
        def run():
            distance = 8 * 2**bit
            shape = (ROWS // (2 * distance), 2, distance, LANES)
            values = adj[...].reshape(shape)
            rates = rate[10 + bit].reshape(shape)
            forwards = fwd[...].reshape(shape)
            term = rates[:, 0] * forwards[:, 0] * (values[:, 1] - values[:, 0])
            others = tuple(other for other in every if other != bit)
            put(10 + bit, *fold(term.reshape(32, 8, LANES), others))

        return run

    def gradient_pair(bit, from_above, from_below):
        has = device_bit(bit).astype(F32)
        lacks = 1.0 - has
        low = rate[bit, lower] * fwd[lower] * (from_above - adj[lower]) * lacks
        theirs = has * from_below - lacks * fwd[upper]
        high = rate[bit, upper] * adj[upper] * theirs
        term = jnp.concatenate([low, high], axis=0)
        put(bit, *fold(term.reshape(64, 8, LANES), every))

    def gradient_cross(number):
        def run():
            bit = CROSS[number][0]
            cross_copy(number, fwd.at[upper], cross_half, h_send, h_recv).wait_recv()
            gradient_pair(bit, cross_half[number], cross_half[number])

        return run

    def gradient_ring(bit, hop):
        def run():
            gradient_pair(bit, ring_a[hop - 1], ring_f[hop - 1])

        return run

    def likelihood():
        zero = [jnp.zeros((8, LANES), F32)] * 6
        logs = counts[...] * jnp.log(fwd[...])
        put(EVENTS, jnp.sum(logs.reshape(64, 8, LANES), axis=0), zero)
        spot = (iota((8, LANES), 0) == 0) & (iota((8, LANES), 1) == 0) & first_device
        put(EVENTS + 1, jnp.where(spot, jnp.log(fwd[0:8]), 0.0), zero)

    sub32 = iota((32, LANES), 0)
    lane32 = iota((32, LANES), 1)
    picker_sub = iota((32, 56), 0)
    picker_lane = iota((32, 56), 1)
    on_total = picker_lane < 8
    sub_part = (picker_lane >> jnp.clip(picker_sub - 7, 0, 2)) & 1
    is_sub = (picker_sub >= 7) & (picker_sub < 10)
    is_row = (picker_sub >= 10) & (picker_sub < 16)
    row_part = (picker_lane >> 3) == picker_sub - 9
    picker = jnp.where(
        is_sub,
        jnp.where(on_total, sub_part, 0),
        jnp.where(is_row, row_part.astype(jnp.int32), on_total.astype(jnp.int32)),
    ).astype(F32)
    lane_part = (lane32 >> jnp.minimum(sub32, 6)) & 1
    device_part = (device >> jnp.clip(sub32 - FIRST_DEVICE_BIT, 0, 8)) & 1
    weights32 = jnp.where(
        sub32 < 7,
        lane_part,
        jnp.where(sub32 < 16, 1, jnp.where(sub32 < EVENTS, device_part, (sub32 == EVENTS).astype(jnp.int32))),
    ).astype(F32)
    lane8 = iota((8, LANES), 1)

    def collect(columns):
        def run():
            tile = reduce_out[0]
            for column in columns:
                at = pl.ds(column * LANES, LANES)
                picked = nn(picker, folded[:, at]) * weights32
                sums = jnp.sum(jnp.where(sub32 == column, 0.0, picked) if column < EVENTS else picked, axis=1, keepdims=True)
                for group in range(4):
                    tile = jnp.where(
                        lane8 == 32 * group + column, sums[8 * group : 8 * group + 8], tile
                    )
            reduce_out[0] = tile

        return run

    reduce_out[0] = jnp.zeros((8, LANES), F32)
    tasks = [gradient_lane(bit) for bit in range(7)]
    tasks += [gradient_sub(bit) for bit in range(3)]
    tasks += [gradient_row(bit) for bit in range(6)]
    tasks += [likelihood]
    tasks += [gradient_cross(number) for number in range(len(CROSS))]
    tasks += [collect((column,)) for column in range(16)]
    tasks += [collect((column,)) for column in (16, 17, 18, 19, 24, 25, 26)]
    tasks += [gradient_ring(20, 1), gradient_ring(21, 2), collect((20,)), collect((21,))]
    late = {6 * PIECES: gradient_ring(22, 4), 6 * PIECES + 1: collect((22,))}
    slots = (HOPS - 1) * PIECES
    done = 0
    for hop in range(1, HOPS + 1):
        for piece in range(PIECES):
            slot = (hop - 1) * PIECES + piece
            goal = -(-len(tasks) * (slot + 1) // (slots - PIECES))
            while done < min(goal, len(tasks)):
                tasks[done]()
                done += 1
            if slot in late:
                late[slot]()
            up_half(hop, piece).wait_recv()
            if hop < HOPS:
                begin(up_half(hop + 1, piece))
            down_half(hop, piece).wait_recv()
            if hop < HOPS:
                begin(down_half(hop + 1, piece))
    gradient_ring(23, 8)()
    collect((23,))()

    for stage, peers in enumerate(STAGES):
        copies = []
        for number, (grp_distances, wide_distances) in enumerate(peers):
            where = {"grp": flip(grp, grp_distances), "wide": flip(wide, wide_distances)}
            copy = remote(
                reduce_out.at[stage],
                reduce_in.at[stage, number],
                r_send.at[stage, number],
                r_recv.at[stage, number],
                where,
            )
            begin(copy)
            copies.append(copy)
        for copy in copies:
            copy.wait_recv()
        total = reduce_out[stage] + reduce_in[stage, 0]
        if len(peers) == 3:
            total = total + (reduce_in[stage, 1] + reduce_in[stage, 2])
        reduce_out[stage + 1] = total

    tile = reduce_out[len(STAGES)]
    spread = jnp.concatenate(
        [tile] + [pltpu.roll(tile, LANES - 32 * group, 1) for group in range(1, 4)], axis=0
    )
    totals = spread[EVENTS : EVENTS + 1, :]
    inside = (sub32 < EVENTS) & (lane32 < EVENTS)
    matrix = jnp.where(inside, spread, 0.0)
    matrix = matrix + jnp.where(inside & (sub32 == lane32), totals, 0.0)
    matrix = jnp.concatenate([matrix, jnp.zeros((LANES - 32, LANES), F32)], axis=0)
    by_event = onehot[...]
    gradient = nt(nt(by_event[0:32], matrix), by_event)
    grad_ref[...] = gradient[0:EVENTS, 0:EVENTS]
    loglik_ref[0, 0] = jnp.sum(jnp.where((sub32 == EVENTS) & (lane32 == EVENTS), spread, 0.0)) / float(
        PATIENTS
    )
    empty_ref[0, 0] = jnp.sum(jnp.where((sub32 == EVENTS) & (lane32 == EVENTS + 1), spread, 0.0))

    for copy in started:
        copy.wait_send()


def body(log_hazards, bit_order, patients, start_dist, start_adjoint):
    vmem = pl.BlockSpec(memory_space=pltpu.VMEM)
    smem = pl.BlockSpec(memory_space=pltpu.SMEM)
    dma = pltpu.SemaphoreType.DMA

    def block(*shape):
        return pltpu.VMEM(shape, F32)

    distribution, gradient, loglik, empty_state = pl.pallas_call(
        kernel,
        out_shape=(
            jax.ShapeDtypeStruct((ROWS, LANES), F32),
            jax.ShapeDtypeStruct((EVENTS, EVENTS), F32),
            jax.ShapeDtypeStruct((1, 1), F32),
            jax.ShapeDtypeStruct((1, 1), F32),
        ),
        in_specs=[vmem, smem, vmem, vmem, vmem],
        out_specs=(vmem, vmem, smem, smem),
        scratch_shapes=[
            block(EVENTS, ROWS, LANES),
            block(ROWS, LANES),
            block(ROWS, LANES),
            block(ROWS, LANES),
            block(ROWS, LANES),
            block(ROWS, LANES),
            block(ROWS, LANES),
            block(56, COLUMNS * LANES),
            block(HOPS, ROWS, LANES),
            block(HOPS, ROWS, LANES),
            block(HOPS, HALF, LANES),
            block(HOPS, HALF, LANES),
            block(len(CROSS), ROWS, LANES),
            block(len(CROSS), HALF, LANES),
            block(len(STAGES) + 1, 8, LANES),
            block(len(STAGES), 3, 8, LANES),
            block(LANES, LANES),
            block(LANES, LANES),
            block(ROWS + 32, LANES),
            dma((HOPS, CHUNKS)),
            dma((HOPS, CHUNKS)),
            dma((HOPS, CHUNKS)),
            dma((HOPS, CHUNKS)),
            dma((HOPS, PIECES)),
            dma((HOPS, PIECES)),
            dma((HOPS, PIECES)),
            dma((HOPS, PIECES)),
            dma((len(CROSS),)),
            dma((len(CROSS),)),
            dma((len(CROSS),)),
            dma((len(CROSS),)),
            dma((len(STAGES), 3)),
            dma((len(STAGES), 3)),
        ],
        compiler_params=pltpu.CompilerParams(
            collective_id=0, has_side_effects=True, vmem_limit_bytes=48 * 2**20
        ),
    )(
        log_hazards,
        bit_order,
        patients.reshape(PATIENTS // LANES, LANES),
        start_dist.reshape(ROWS, LANES),
        start_adjoint.reshape(ROWS, LANES),
    )
    return distribution.reshape(-1), loglik.reshape(()), gradient, empty_state.reshape(())


def solution(mesh):
    return jax.shard_map(
        body,
        mesh=mesh,
        in_specs=(P(), P(), P(), P(("wide", "grp")), P(("wide", "grp"))),
        out_specs=(P(("wide", "grp")), P(), P(), P()),
        check_vma=False,
    )
```

time: 470 us -> 119 us (0.25)
  starting transfers between devices: 115 us -> 0 us
  other arithmetic: 114 us -> 0 us
  Pallas kernels: 0 us -> 110 us
  blocking collectives: 98.9 us -> 0 us
  matrix products: 61.7 us -> 0 us
  local copies, waits for them, and re-layouts: 56.2 us -> 4.61 us
  waiting for transfers between devices: 10.4 us -> 0 us
  between operations: 11 us -> 4.17 us
    pallas_call x0 -> x1, Pallas kernels: none -> 110 us  [body(): pl.pallas_call(kernel, out_shape=(jax.ShapeDtypeStruct((ROWS, LANES), F32...]
    psum x1 -> x0, blocking collectives: 98.9 us -> none  [body(): lax.psum((partial_grad, log_sum, log_first), ('wide', 'grp'))]
    ppermute x15 -> x0, starting transfers between devices: 68.5 us -> none  [partner_2(): return lax.ppermute(value, axis, pairs)]
    dot_general x88 -> x0, matrix products: 61.7 us -> none  [the longest x25 20.8 us: feature_row(): return jnp.dot(listed, to_global, precision=highest) + whole * own_column]
    mul x32 -> x0, other arithmetic: 53.2 us -> none  [the longest x13 18.7 us: local_pull(): rates[:, 0] * others[:, 1]]
    all_to_all x6 -> x0, starting transfers between devices: 46.2 us -> none  [the longest x4 29.7 us: regroup(): lax.all_to_all(three_way, 'grp', split_axis=0, concat_axis=0, tiled=True)]
    another operation x45 -> x0, local copies, waits for them, and re-layouts: 34.8 us -> none  [the longest x26 20.4 us: join_rows(): paired = jnp.stack([lower_half, upper_half], axis=1)]
    add x13 -> x0, other arithmetic: 22.9 us -> none  [the longest x4 21.3 us: rate_of(): offsets[position] + by_row[:, position][:, None]]
  transfers between devices with their start and end apart: 21 -> 0, of which waited for: 2 -> 0; matrix products, arithmetic and copies ran while one was open for 31% -> 0% of each run, Pallas kernels for 0% -> 0%
where the time goes in v1:
time: 119 us
  Pallas kernels  110 us (92%)
  local copies, waits for them, and re-layouts  4.61 us (4%)
  between operations  4.17 us (4%)
    pallas_call x1, Pallas kernels, body(): pl.pallas_call(kernel, out_shape=(jax.ShapeDtypeStruct((ROWS, LANES), F32...  110 us
    unnamed x12, local copies, waits for them, and re-layouts  4.61 us

profile of v1, /device:TPU:1, one launch (start us, length us, event | category | flops | bytes accessed | tf_op | source)
XLA Modules:
  0.0 118.6 jit_solution(18439305403347283277)
XLA Ops:
  0.6 0.0 copy-start.3
  0.6 0.0 copy-start.4
  0.7 0.7 copy-done.3
  1.3 0.0 copy-done.4
  1.3 0.0 copy-start
  1.3 0.9 copy-done
  2.3 0.0 copy-start.1
  2.3 0.9 copy-done.1
  3.2 0.0 copy-start.2
  3.2 0.7 copy-done.2
  3.9 109.8 %shard_map.84 = (f32[512,128]{1,0:T(8,128)S(1)}, f32[25,25]{1,0:T(8,128)S(1)}, f32[1,1]{1,0:T(1,128)}, f32[1,1]{1,0:T(1,128)}) custom-call(f32[25,25]{1,0:T(8,128)S(1)} %copy-done.2, s32[25]{0:T(128)S(1)} %copy-done.4, s32[2,128]{1,0:T(2,128)S(1)} %bitcast.9, f32[512,128]{1,0:T(8,128)S(1)} %bitcast.6, f32[512,128]{1,0:T(8,128)S(1)} %bitcast.7), custom_call_target="tpu_custom_call" | custom-call | tf_op jit(solution)/shard_map/pallas_call | solution.py:629
  113.8 0.7 copy.13
  115.1 0.6 copy.15
Async XLA Ops:
  0.6 0.7 copy-start.3
  0.6 0.7 copy-start.4
  1.3 1.0 copy-start
  2.3 0.9 copy-start.1
  3.2 0.7 copy-start.2

commit v2 on v1

--- a/solution.py
+++ b/solution.py
@@ -16,8 +16,7 @@
 HALF = 256
 CHUNK = 128
 CHUNKS = 4
-PIECE = 64
-PIECES = 4
+PIECES = 2
 HOPS = 8
 FIRST_DEVICE_BIT = 16
 Z_BITS = ((20, 1), (21, 2), (22, 4), (23, 8))
@@ -26,9 +25,9 @@
     (((1,), ()),),
     (((2,), ()), ((), (16,)), ((2,), (16,))),
     (((4,), ()), ((8,), ()), ((4, 8), ())),
-    (((), (1,)), ((), (2,)), ((), (1, 2))),
-    (((), (4,)), ((), (8,)), ((), (4, 8))),
+    tuple(((), tuple(2**bit for bit in range(4) if mask >> bit & 1)) for mask in range(1, 16)),
 )
+PEERS = max(len(peers) for peers in STAGES)
 COLUMNS = EVENTS + 2
 UP_ORDER = (0, 2, 1, 3)
 DOWN_ORDER = (0, 1, 2, 3)
@@ -57,15 +56,20 @@
 
 
 def kernel(
+    hazards_hbm,
+    order_hbm,
+    patients_hbm,
+    p_hbm,
+    q_hbm,
+    dist_ref,
+    grad_ref,
+    loglik_ref,
+    empty_ref,
     hazards_ref,
     order_ref,
     patients_ref,
     p_ref,
     q_ref,
-    dist_ref,
-    grad_ref,
-    loglik_ref,
-    empty_ref,
     rate,
     inverse,
     sum_f,
@@ -76,8 +80,7 @@
     folded,
     ring_p,
     ring_q,
-    ring_f,
-    ring_a,
+    half_in,
     cross_in,
     cross_half,
     reduce_out,
@@ -89,16 +92,15 @@
     p_recv,
     q_send,
     q_recv,
-    f_send,
-    f_recv,
-    a_send,
-    a_recv,
+    z_send,
+    z_recv,
     x_send,
     x_recv,
     h_send,
     h_recv,
     r_send,
     r_recv,
+    local_sem,
 ):
     wide = lax.axis_index("wide")
     grp = lax.axis_index("grp")
@@ -123,6 +125,21 @@
             device_id_type=MESH,
         )
 
+    local_copies = [
+        pltpu.make_async_copy(source, target, local_sem.at[number])
+        for number, (source, target) in enumerate(
+            (
+                (hazards_hbm, hazards_ref),
+                (order_hbm, order_ref),
+                (patients_hbm, patients_ref),
+                (p_hbm, p_ref),
+                (q_hbm, q_ref),
+            )
+        )
+    ]
+    for copy in local_copies:
+        copy.start()
+
     barrier = pltpu.get_barrier_semaphore()
     neighbours = [above, below] + [partner(axis, distance) for _, axis, distance in CROSS]
     for neighbour in neighbours:
@@ -136,34 +153,74 @@
 
     def up_copy(hop, chunk):
         rows = rows_of(chunk)
-        source = p_ref.at[rows] if hop == 1 else ring_p.at[hop - 2, rows]
+        source = p_hbm.at[rows] if hop == 1 else ring_p.at[hop - 2, rows]
         return remote(
             source, ring_p.at[hop - 1, rows], p_send.at[hop - 1, chunk], p_recv.at[hop - 1, chunk], above
         )
 
     def down_copy(hop, chunk):
         rows = rows_of(chunk)
-        source = q_ref.at[rows] if hop == 1 else ring_q.at[hop - 2, rows]
+        source = q_hbm.at[rows] if hop == 1 else ring_q.at[hop - 2, rows]
         return remote(
             source, ring_q.at[hop - 1, rows], q_send.at[hop - 1, chunk], q_recv.at[hop - 1, chunk], below
         )
 
-    def up_half(hop, piece):
-        rows = pl.ds(piece * PIECE, PIECE)
-        if hop == 1:
-            source = fwd.at[pl.ds(HALF + piece * PIECE, PIECE)]
-        else:
-            source = ring_f.at[hop - 2, rows]
+    odd = place % 2
+    step_up = 2 * odd - 1
+
+    def z_rows(piece):
+        return pl.ds(piece * CHUNK, CHUNK)
+
+    def z_copy(source, bit, piece, send, offset):
         return remote(
-            source, ring_f.at[hop - 1, rows], f_send.at[hop - 1, piece], f_recv.at[hop - 1, piece], above
+            source,
+            half_in.at[bit, z_rows(piece)],
+            z_send.at[send, piece],
+            z_recv.at[bit, piece],
+            {"wide": wide - place + (place + offset + 16) % 16},
         )
 
-    def down_half(hop, piece):
-        rows = pl.ds(piece * PIECE, PIECE)
-        source = adj.at[rows] if hop == 1 else ring_a.at[hop - 2, rows]
-        return remote(
-            source, ring_a.at[hop - 1, rows], a_send.at[hop - 1, piece], a_recv.at[hop - 1, piece], below
-        )
+    guarded = []
+
+    def begin_if(condition, copy):
+        @pl.when(condition)
+        def _():
+            copy.start()
+
+        guarded.append((condition, copy))
+
+    def forward_piece(piece):
+        return fwd.at[pl.ds(HALF + piece * CHUNK, CHUNK)]
+
+    def adjoint_piece(piece):
+        return adj.at[z_rows(piece)]
+
+    def differs(bit):
+        return (place // 2**bit) % 2 != odd
+
+    def send_forward(piece):
+        source = forward_piece(piece)
+        begin_if(odd == 0, z_copy(source, 0, piece, 0, 1))
+        begin_if((place // 8) % 2 == 0, z_copy(source, 3, piece, 1, 8))
+        for bit in (2, 1):
+            begin_if(differs(bit) & (odd == 1), z_copy(source, bit, piece, 1 + bit, 2**bit))
+
+    def send_adjoint(piece):
+        source = adjoint_piece(piece)
+        begin_if(odd == 1, z_copy(source, 0, piece, 0, -1))
+        begin_if((place // 8) % 2 == 1, z_copy(source, 3, piece, 1, -8))
+        for bit in (2, 1):
+            begin_if(differs(bit) & (odd == 0), z_copy(source, bit, piece, 1 + bit, -(2**bit)))
+
+    def relay(piece):
+        source = half_in.at[0, z_rows(piece)]
+        for bit in (2, 1):
+            begin_if(
+                differs(bit), z_copy(source, bit, piece, 3 + bit, step_up * (2**bit - 1))
+            )
+
+    def z_wait(bit, piece):
+        z_copy(adjoint_piece(piece), bit, piece, 0, 1).wait_recv()
 
     def begin(copy):
         copy.start()
@@ -189,7 +246,7 @@
 
             started.append(cross_copy(number, low, target, send, receive))
 
-    cross_start(p_ref, q_ref, cross_in, x_send, x_recv)
+    cross_start(p_hbm, q_hbm, cross_in, x_send, x_recv)
 
     lane_id = iota((1, LANES), 1)
     lane_has = [((lane_id >> bit) & 1).astype(F32) for bit in range(7)]
@@ -350,7 +407,7 @@
     def add_cross(number):
         def run():
             bit = CROSS[number][0]
-            cross_copy(number, p_ref, cross_in, x_send, x_recv).wait_recv()
+            cross_copy(number, p_hbm, cross_in, x_send, x_recv).wait_recv()
             add_pair(bit, cross_in.at[number], cross_in.at[number])
 
         return run
@@ -361,7 +418,11 @@
 
         return run
 
-    tasks = [make_tables]
+    def land():
+        for copy in local_copies:
+            copy.wait()
+
+    tasks = [land, make_tables]
     tasks += [make_rate(bit) for bit in range(EVENTS)]
     tasks += [make_counts]
     for chunk in range(CHUNKS):
@@ -412,8 +473,7 @@
         up_copy(HOPS, up).wait_recv()
         finish_forward(up)
         if up >= 2:
-            for piece in (2 * up - 4, 2 * up - 3):
-                begin(up_half(1, piece))
+            send_forward(up - 2)
         down_copy(HOPS, down).wait_recv()
         ready = [c for c in DOWN_ORDER[: step + 1] if c in UP_ORDER[: step + 1]]
         before = [c for c in DOWN_ORDER[:step] if c in UP_ORDER[:step]]
@@ -421,8 +481,7 @@
             if chunk not in before:
                 finish_adjoint(chunk)
                 if chunk < 2:
-                    for piece in (2 * chunk, 2 * chunk + 1):
-                        begin(down_half(1, piece))
+                    send_adjoint(chunk)
 
     upper = pl.ds(HALF, HALF)
     lower = pl.ds(0, HALF)
@@ -496,11 +555,19 @@
 
         return run
 
-    def gradient_ring(bit, hop):
-        def run():
-            gradient_pair(bit, ring_a[hop - 1], ring_f[hop - 1])
-
-        return run
+    def gradient_ring(bit):
+        def run():
+            if bit:
+                for piece in range(PIECES):
+                    z_wait(bit, piece)
+            gradient_pair(20 + bit, half_in[bit], half_in[bit])
+
+        return run
+
+    def relay_all():
+        for piece in range(PIECES):
+            z_wait(0, piece)
+            relay(piece)
 
     def likelihood():
         zero = [jnp.zeros((8, LANES), F32)] * 6
@@ -548,34 +615,19 @@
         return run
 
     reduce_out[0] = jnp.zeros((8, LANES), F32)
-    tasks = [gradient_lane(bit) for bit in range(7)]
+    tasks = [gradient_lane(bit) for bit in range(5)]
+    tasks += [relay_all]
+    tasks += [gradient_lane(bit) for bit in range(5, 7)]
     tasks += [gradient_sub(bit) for bit in range(3)]
     tasks += [gradient_row(bit) for bit in range(6)]
-    tasks += [likelihood]
+    tasks += [likelihood, gradient_ring(0)]
+    tasks += [collect(tuple(range(16)) + (20, 25, 26))]
     tasks += [gradient_cross(number) for number in range(len(CROSS))]
-    tasks += [collect((column,)) for column in range(16)]
-    tasks += [collect((column,)) for column in (16, 17, 18, 19, 24, 25, 26)]
-    tasks += [gradient_ring(20, 1), gradient_ring(21, 2), collect((20,)), collect((21,))]
-    late = {6 * PIECES: gradient_ring(22, 4), 6 * PIECES + 1: collect((22,))}
-    slots = (HOPS - 1) * PIECES
-    done = 0
-    for hop in range(1, HOPS + 1):
-        for piece in range(PIECES):
-            slot = (hop - 1) * PIECES + piece
-            goal = -(-len(tasks) * (slot + 1) // (slots - PIECES))
-            while done < min(goal, len(tasks)):
-                tasks[done]()
-                done += 1
-            if slot in late:
-                late[slot]()
-            up_half(hop, piece).wait_recv()
-            if hop < HOPS:
-                begin(up_half(hop + 1, piece))
-            down_half(hop, piece).wait_recv()
-            if hop < HOPS:
-                begin(down_half(hop + 1, piece))
-    gradient_ring(23, 8)()
-    collect((23,))()
+    tasks += [collect((16, 17, 18, 19, 24))]
+    for bit in (1, 2, 3):
+        tasks += [gradient_ring(bit), collect((20 + bit,))]
+    for task in tasks:
+        task()
 
     for stage, peers in enumerate(STAGES):
         copies = []
@@ -592,10 +644,10 @@
             copies.append(copy)
         for copy in copies:
             copy.wait_recv()
-        total = reduce_out[stage] + reduce_in[stage, 0]
-        if len(peers) == 3:
-            total = total + (reduce_in[stage, 1] + reduce_in[stage, 2])
-        reduce_out[stage + 1] = total
+        parts = [reduce_out[stage]] + [reduce_in[stage, number] for number in range(len(peers))]
+        while len(parts) > 1:
+            parts = [low + high for low, high in zip(parts[0::2], parts[1::2])]
+        reduce_out[stage + 1] = parts[0]
 
     tile = reduce_out[len(STAGES)]
     spread = jnp.concatenate(
@@ -616,6 +668,11 @@
 
     for copy in started:
         copy.wait_send()
+    for condition, copy in guarded:
+
+        @pl.when(condition)
+        def _():
+            copy.wait_send()
 
 
 def body(log_hazards, bit_order, patients, start_dist, start_adjoint):
@@ -634,9 +691,14 @@
             jax.ShapeDtypeStruct((1, 1), F32),
             jax.ShapeDtypeStruct((1, 1), F32),
         ),
-        in_specs=[vmem, smem, vmem, vmem, vmem],
+        in_specs=[pl.BlockSpec(memory_space=pl.ANY)] * 5,
         out_specs=(vmem, vmem, smem, smem),
         scratch_shapes=[
+            block(EVENTS, EVENTS),
+            pltpu.SMEM((EVENTS,), jnp.int32),
+            pltpu.VMEM((PATIENTS // LANES, LANES), jnp.int32),
+            block(ROWS, LANES),
+            block(ROWS, LANES),
             block(EVENTS, ROWS, LANES),
             block(ROWS, LANES),
             block(ROWS, LANES),
@@ -647,12 +709,11 @@
             block(56, COLUMNS * LANES),
             block(HOPS, ROWS, LANES),
             block(HOPS, ROWS, LANES),
-            block(HOPS, HALF, LANES),
-            block(HOPS, HALF, LANES),
+            block(4, HALF, LANES),
             block(len(CROSS), ROWS, LANES),
             block(len(CROSS), HALF, LANES),
             block(len(STAGES) + 1, 8, LANES),
-            block(len(STAGES), 3, 8, LANES),
+            block(len(STAGES), PEERS, 8, LANES),
             block(LANES, LANES),
             block(LANES, LANES),
             block(ROWS + 32, LANES),
@@ -660,19 +721,18 @@
             dma((HOPS, CHUNKS)),
             dma((HOPS, CHUNKS)),
             dma((HOPS, CHUNKS)),
-            dma((HOPS, PIECES)),
-            dma((HOPS, PIECES)),
-            dma((HOPS, PIECES)),
-            dma((HOPS, PIECES)),
+            dma((6, PIECES)),
+            dma((4, PIECES)),
             dma((len(CROSS),)),
             dma((len(CROSS),)),
             dma((len(CROSS),)),
             dma((len(CROSS),)),
-            dma((len(STAGES), 3)),
-            dma((len(STAGES), 3)),
+            dma((len(STAGES), PEERS)),
+            dma((len(STAGES), PEERS)),
+            dma((5,)),
         ],
         compiler_params=pltpu.CompilerParams(
-            collective_id=0, has_side_effects=True, vmem_limit_bytes=48 * 2**20
+            collective_id=0, has_side_effects=True, vmem_limit_bytes=60 * 2**20
         ),
     )(
         log_hazards,

time: 119 us -> 111 us (0.933)
  Pallas kernels: 110 us -> 104 us
  local copies, waits for them, and re-layouts: 4.61 us -> 2.29 us
    pallas_call x1, Pallas kernels: 110 us -> 104 us  [body(): pl.pallas_call(kernel, out_shape=(jax.ShapeDtypeStruct((ROWS, LANES), F32...]
    unnamed x12 -> x4, local copies, waits for them, and re-layouts: 4.61 us -> 2.29 us
where the time goes in v2:
time: 111 us
  Pallas kernels  104 us (94%)
  between operations  4.3 us (4%)
  local copies, waits for them, and re-layouts  2.29 us (2%)
    pallas_call x1, Pallas kernels, body(): pl.pallas_call(kernel, out_shape=(jax.ShapeDtypeStruct((ROWS, LANES), F32...  104 us
    unnamed x4, local copies, waits for them, and re-layouts  2.29 us

profile of v2, /device:TPU:1, one launch (start us, length us, event | category | flops | bytes accessed | tf_op | source)
XLA Modules:
  0.0 110.7 jit_solution(7638293805794864528)
XLA Ops:
  0.6 104.1 %shard_map.84 = (f32[512,128]{1,0:T(8,128)}, f32[25,25]{1,0:T(8,128)}, f32[1,1]{1,0:T(1,128)}, f32[1,1]{1,0:T(1,128)}) custom-call(f32[25,25]{1,0:T(8,128)} %hazards_hbm.1, s32[25]{0:T(128)} %order_hbm.1, s32[2,128]{1,0:T(2,128)} %bitcast.9, f32[512,128]{1,0:T(8,128)} %bitcast.6, f32[512,128]{1,0:T(8,128)} %bitcast.7), custom_call_target="tpu_custom_call" | custom-call | tf_op jit(solution)/shard_map/pallas_call | solution.py:686
  104.7 0.0 copy-start
  104.7 1.7 %copy.13 = f32[65536]{0:T(1024)} copy(f32[65536]{0:T(1024)} %bitcast.8) | data formatting | bytes 524288
  107.1 0.0 copy-done
  107.1 0.6 copy.15
Async XLA Ops:
  104.7 2.4 %copy-start = (f32[25,25]{1,0:T(8,128)S(1)}, f32[25,25]{1,0:T(8,128)}, u32[]{:S(2)}) copy-start(f32[25,25]{1,0:T(8,128)} %get-tuple-element.18) | copy-start | bytes 7504

commit v3 on v2

--- a/solution.py
+++ b/solution.py
@@ -17,9 +17,7 @@
 CHUNK = 128
 CHUNKS = 4
 PIECES = 2
-HOPS = 8
 FIRST_DEVICE_BIT = 16
-Z_BITS = ((20, 1), (21, 2), (22, 4), (23, 8))
 CROSS = ((16, "grp", 1), (17, "grp", 2), (18, "grp", 4), (19, "grp", 8), (24, "wide", 16))
 STAGES = (
     (((1,), ()),),
@@ -29,8 +27,7 @@
 )
 PEERS = max(len(peers) for peers in STAGES)
 COLUMNS = EVENTS + 2
-UP_ORDER = (0, 2, 1, 3)
-DOWN_ORDER = (0, 1, 2, 3)
+ORDER = (0, 2, 1, 3)
 
 
 def nn(left, right):
@@ -78,8 +75,11 @@
     adj,
     counts,
     folded,
-    ring_p,
-    ring_q,
+    z_in,
+    merge_in,
+    wrap_in,
+    merged,
+    factor,
     half_in,
     cross_in,
     cross_half,
@@ -90,8 +90,7 @@
     tables,
     p_send,
     p_recv,
-    q_send,
-    q_recv,
+    m_recv,
     z_send,
     z_recv,
     x_send,
@@ -106,8 +105,9 @@
     grp = lax.axis_index("grp")
     device = wide * 16 + grp
     place = wide % 16
-    above = {"wide": wide - place + (place + 1) % 16}
-    below = {"wide": wide - place + (place + 15) % 16}
+
+    def to_place(offset):
+        return {"wide": wide - place + (place + offset + 16) % 16}
 
     def device_bit(bit):
         return (device // 2 ** (bit - FIRST_DEVICE_BIT)) % 2
@@ -141,7 +141,8 @@
         copy.start()
 
     barrier = pltpu.get_barrier_semaphore()
-    neighbours = [above, below] + [partner(axis, distance) for _, axis, distance in CROSS]
+    neighbours = [to_place(offset) for offset in (-4, -3, -2, -1, 1, 2, 3, 4)]
+    neighbours += [partner(axis, distance) for _, axis, distance in CROSS]
     for neighbour in neighbours:
         pl.semaphore_signal(barrier, inc=1, device_id=neighbour, device_id_type=MESH)
     pl.semaphore_wait(barrier, len(neighbours))
@@ -150,20 +151,6 @@
 
     def rows_of(chunk):
         return pl.ds(chunk * CHUNK, CHUNK)
-
-    def up_copy(hop, chunk):
-        rows = rows_of(chunk)
-        source = p_hbm.at[rows] if hop == 1 else ring_p.at[hop - 2, rows]
-        return remote(
-            source, ring_p.at[hop - 1, rows], p_send.at[hop - 1, chunk], p_recv.at[hop - 1, chunk], above
-        )
-
-    def down_copy(hop, chunk):
-        rows = rows_of(chunk)
-        source = q_hbm.at[rows] if hop == 1 else ring_q.at[hop - 2, rows]
-        return remote(
-            source, ring_q.at[hop - 1, rows], q_send.at[hop - 1, chunk], q_recv.at[hop - 1, chunk], below
-        )
 
     odd = place % 2
     step_up = 2 * odd - 1
@@ -226,9 +213,104 @@
         copy.start()
         started.append(copy)
 
-    for up, down in zip(UP_ORDER, DOWN_ORDER):
-        begin(up_copy(1, up))
-        begin(down_copy(1, down))
+    top = (place // 8) % 2
+    middle = top != (place // 4) % 2
+    end = top == (place // 4) % 2
+    toward = 4 - 8 * top
+
+    def first_copy(source, bit, chunk, send, offset):
+        rows = rows_of(chunk)
+        return remote(
+            source, z_in.at[bit, rows], p_send.at[send, chunk], p_recv.at[bit, chunk], to_place(offset)
+        )
+
+    def first_wait(bit, chunk):
+        first_copy(p_hbm.at[rows_of(chunk)], bit, chunk, 0, 1).wait_recv()
+
+    def half_rows(chunk):
+        return pl.ds((chunk % 2) * CHUNK, CHUNK)
+
+    def first_leg(source, chunk, side):
+        if chunk < 2:
+            target, semaphore, offset = merge_in.at[half_rows(chunk)], m_recv.at[0, chunk], toward
+        else:
+            target, semaphore, offset = wrap_in.at[side, half_rows(chunk)], m_recv.at[side, chunk], -toward
+        return remote(source, target, p_send.at[5, chunk], semaphore, to_place(offset))
+
+    def start_far(chunk):
+        rows = rows_of(chunk)
+        for value, source in ((0, p_hbm.at[rows]), (1, q_hbm.at[rows])):
+            ready = (top == value) & middle if chunk < 2 else top == value
+            begin_if(ready, first_leg(source, chunk, value))
+
+    def start_neighbour(chunk):
+        rows = rows_of(chunk)
+        begin_if(odd == 0, first_copy(p_hbm.at[rows], 0, chunk, 0, 1))
+        begin_if(odd == 1, first_copy(q_hbm.at[rows], 0, chunk, 0, -1))
+
+    def start_own(chunk):
+        rows = rows_of(chunk)
+        for bit in (2, 1):
+            wanted = differs(bit) & end if bit == 2 and chunk < 2 else differs(bit)
+            begin_if(wanted & (odd == 1), first_copy(p_hbm.at[rows], bit, chunk, bit, 2**bit))
+            begin_if(wanted & (odd == 0), first_copy(q_hbm.at[rows], bit, chunk, bit, -(2**bit)))
+
+    for chunk in ORDER:
+        start_far(chunk)
+    for chunk in ORDER:
+        start_neighbour(chunk)
+    for chunk in ORDER:
+        start_own(chunk)
+
+    def pass_neighbour(chunk):
+        def run():
+            first_wait(0, chunk)
+            source = z_in.at[0, rows_of(chunk)]
+            for bit in (2, 1):
+                wanted = differs(bit) & end if bit == 2 and chunk < 2 else differs(bit)
+                begin_if(wanted, first_copy(source, bit, chunk, 2 + bit, step_up * (2**bit - 1)))
+
+        return run
+
+    def pass_wrap(chunk):
+        def run():
+            rows = half_rows(chunk)
+            for side, offset in ((0, -4), (1, 4)):
+                source = wrap_in.at[side, rows]
+
+                @pl.when(end)
+                def _():
+                    remote(
+                        source, source, p_send.at[5, chunk], m_recv.at[side, chunk], to_place(4)
+                    ).wait_recv()
+
+                begin_if(end, first_copy(source, 3, chunk, 6 + side, offset))
+
+        return run
+
+    def pass_merged(chunk):
+        def run():
+            rows = rows_of(chunk)
+            source = merge_in.at[rows]
+
+            @pl.when(middle)
+            def _():
+                remote(source, source, p_send.at[5, chunk], m_recv.at[0, chunk], to_place(4)).wait_recv()
+                high = top.astype(F32)
+                own = high * p_ref[rows] + (1.0 - high) * q_ref[rows]
+                far = rate[23, rows] * factor[0:1, :] * merge_in[rows]
+                merged[rows] = far + rate[22, rows] * own
+
+            begin_if(middle, first_copy(merged.at[rows], 2, chunk, 7, -toward))
+
+        return run
+
+    def pass_second(chunk):
+        def run():
+            first_wait(2, chunk)
+            begin_if(middle, first_copy(z_in.at[2, rows_of(chunk)], 3, chunk, 6, toward))
+
+        return run
 
     def cross_copy(number, source, target, send, receive):
         _, axis, distance = CROSS[number]
@@ -274,6 +356,8 @@
         same = sub == lane
         diagonal = jnp.sum(jnp.where(same, matrix, 0.0), axis=1, keepdims=True)
         coupling = jnp.where(same, 0.0, matrix)
+        sign = (2 * top - 1).astype(F32)
+        factor[...] = jnp.broadcast_to(jnp.exp(coupling[23:24, 22:23] * sign), (8, LANES))
         lane_bits = jnp.where(sub < 7, (lane >> jnp.minimum(sub, 7)) & 1, 0).astype(F32)
         tables[ROWS : ROWS + 32, :] = jnp.exp(nn(coupling[0:32], lane_bits))
         row = iota((ROWS, LANES), 0)
@@ -399,22 +483,17 @@
             )
         counts[...] = total
 
-    def add_pair(bit, up, down):
+    def add_pair(bit, received):
         has = device_bit(bit).astype(F32)
-        sum_f[...] += rate[bit] * up[...] * has
-        sum_a[...] += rate[bit] * down[...] * (1.0 - has)
+        term = rate[bit] * received[...]
+        sum_f[...] += term * has
+        sum_a[...] += term * (1.0 - has)
 
     def add_cross(number):
         def run():
             bit = CROSS[number][0]
             cross_copy(number, p_hbm, cross_in, x_send, x_recv).wait_recv()
-            add_pair(bit, cross_in.at[number], cross_in.at[number])
-
-        return run
-
-    def add_ring(bit, hop):
-        def run():
-            add_pair(bit, ring_p.at[hop - 1], ring_q.at[hop - 1])
+            add_pair(bit, cross_in.at[number])
 
         return run
 
@@ -422,36 +501,66 @@
         for copy in local_copies:
             copy.wait()
 
-    tasks = [land, make_tables]
-    tasks += [make_rate(bit) for bit in range(EVENTS)]
+    def add_first():
+        for chunk in ORDER:
+            first_wait(1, chunk)
+        add_pair(20, z_in.at[0])
+        add_pair(21, z_in.at[1])
+
+    @pl.when(end)
+    def _():
+        z_in[3, 0:HALF] = jnp.zeros((HALF, LANES), F32)
+
+    tasks = [land, make_tables, make_rate(22), make_rate(23)]
+    tasks += [make_rate(bit) for bit in range(EVENTS) if bit not in (22, 23)]
     tasks += [make_counts]
     for chunk in range(CHUNKS):
         tasks += [make_inverse(chunk), local_forward(chunk), local_adjoint(chunk)]
     tasks += [add_cross(number) for number in range(len(CROSS))]
-    tasks += [add_ring(20, 1), add_ring(21, 2)]
-    slots = (HOPS - 1) * CHUNKS
-    late = {5 * CHUNKS: add_ring(22, 4)}
+    services = [
+        pass_wrap(2),
+        pass_merged(0),
+        pass_wrap(3),
+        pass_merged(1),
+        pass_neighbour(0),
+        pass_neighbour(2),
+        pass_neighbour(1),
+        pass_neighbour(3),
+        pass_second(0),
+        pass_second(1),
+    ]
     done = 0
-    for hop in range(1, HOPS):
-        for step, (up, down) in enumerate(zip(UP_ORDER, DOWN_ORDER)):
-            slot = (hop - 1) * CHUNKS + step
-            goal = -(-len(tasks) * (slot + 1) // (slots - CHUNKS))
-            while done < min(goal, len(tasks)):
-                tasks[done]()
-                done += 1
-            if slot in late:
-                late[slot]()
-            up_copy(hop, up).wait_recv()
-            begin(up_copy(hop + 1, up))
-            down_copy(hop, down).wait_recv()
-            begin(down_copy(hop + 1, down))
+    for number, service in enumerate(services):
+        goal = max(6, len(tasks) * (number + 1) // (len(services) + 1))
+        while done < goal:
+            tasks[done]()
+            done += 1
+        service()
+    while done < len(tasks):
+        tasks[done]()
+        done += 1
+    add_first()
 
     first_device = device == 0
 
-    def finish_forward(chunk):
+    def finish(chunk):
         rows = rows_of(chunk)
-        has = device_bit(23).astype(F32)
-        total = sum_f[rows] + rate[23, rows] * ring_p[HOPS - 1, rows] * has
+        if chunk < 2:
+
+            @pl.when(middle)
+            def _():
+                first_wait(3, chunk)
+
+        else:
+            first_wait(2, chunk)
+            first_wait(3, chunk)
+        has2 = device_bit(22).astype(F32)
+        has3 = device_bit(23).astype(F32)
+        part2 = rate[22, rows] * z_in[2, rows]
+        if chunk < 2:
+            part2 = jnp.where(middle, part2, z_in[2, rows])
+        part3 = rate[23, rows] * z_in[3, rows]
+        total = sum_f[rows] + part2 * has2 + part3 * has3
         if chunk == 0:
             spot = (iota((CHUNK, LANES), 0) == 0) & (iota((CHUNK, LANES), 1) == 0) & first_device
             total = total + jnp.where(spot, float(2**EVENTS), 0.0)
@@ -461,27 +570,16 @@
             values = total * inverse[rows]
             dist_ref[rows] = values
         fwd[rows] = values
-
-    def finish_adjoint(chunk):
-        rows = rows_of(chunk)
-        lacks = 1.0 - device_bit(23).astype(F32)
-        total = sum_a[rows] + rate[23, rows] * ring_q[HOPS - 1, rows] * lacks
-        weights = counts[rows] / (float(PATIENTS) * fwd[rows])
-        adj[rows] = (weights + total * 2.0**-12) * inverse[rows]
-
-    for step, (up, down) in enumerate(zip(UP_ORDER, DOWN_ORDER)):
-        up_copy(HOPS, up).wait_recv()
-        finish_forward(up)
-        if up >= 2:
-            send_forward(up - 2)
-        down_copy(HOPS, down).wait_recv()
-        ready = [c for c in DOWN_ORDER[: step + 1] if c in UP_ORDER[: step + 1]]
-        before = [c for c in DOWN_ORDER[:step] if c in UP_ORDER[:step]]
-        for chunk in ready:
-            if chunk not in before:
-                finish_adjoint(chunk)
-                if chunk < 2:
-                    send_adjoint(chunk)
+        pulled = sum_a[rows] + part2 * (1.0 - has2) + part3 * (1.0 - has3)
+        weights = counts[rows] / (float(PATIENTS) * values)
+        adj[rows] = (weights + pulled * 2.0**-12) * inverse[rows]
+
+    for chunk in (2, 3, 0, 1):
+        finish(chunk)
+        if chunk < 2:
+            send_adjoint(chunk)
+        else:
+            send_forward(chunk - 2)
 
     upper = pl.ds(HALF, HALF)
     lower = pl.ds(0, HALF)
@@ -707,8 +805,11 @@
             block(ROWS, LANES),
             block(ROWS, LANES),
             block(56, COLUMNS * LANES),
-            block(HOPS, ROWS, LANES),
-            block(HOPS, ROWS, LANES),
+            block(4, ROWS, LANES),
+            block(HALF, LANES),
+            block(2, HALF, LANES),
+            block(HALF, LANES),
+            block(8, LANES),
             block(4, HALF, LANES),
             block(len(CROSS), ROWS, LANES),
             block(len(CROSS), HALF, LANES),
@@ -717,10 +818,9 @@
             block(LANES, LANES),
             block(LANES, LANES),
             block(ROWS + 32, LANES),
-            dma((HOPS, CHUNKS)),
-            dma((HOPS, CHUNKS)),
-            dma((HOPS, CHUNKS)),
-            dma((HOPS, CHUNKS)),
+            dma((8, CHUNKS)),
+            dma((4, CHUNKS)),
+            dma((2, CHUNKS)),
             dma((6, PIECES)),
             dma((4, PIECES)),
             dma((len(CROSS),)),

time: 111 us -> 109 us (0.982)
  Pallas kernels: 104 us -> 102 us
    pallas_call x1, Pallas kernels: 104 us -> 102 us  [body(): pl.pallas_call(kernel, out_shape=(jax.ShapeDtypeStruct((ROWS, LANES), F32...]
where the time goes in v3:
time: 109 us
  Pallas kernels  102 us (94%)
  between operations  4.3 us (4%)
  local copies, waits for them, and re-layouts  2.29 us (2%)
    pallas_call x1, Pallas kernels, body(): pl.pallas_call(kernel, out_shape=(jax.ShapeDtypeStruct((ROWS, LANES), F32...  102 us
    unnamed x4, local copies, waits for them, and re-layouts  2.29 us

profile of v3, /device:TPU:1, one launch (start us, length us, event | category | flops | bytes accessed | tf_op | source)
XLA Modules:
  0.0 108.9 jit_solution(15913199789533234581)
XLA Ops:
  0.6 102.3 %shard_map.84 = (f32[512,128]{1,0:T(8,128)}, f32[25,25]{1,0:T(8,128)}, f32[1,1]{1,0:T(1,128)}, f32[1,1]{1,0:T(1,128)}) custom-call(f32[25,25]{1,0:T(8,128)} %hazards_hbm.1, s32[25]{0:T(128)} %order_hbm.1, s32[2,128]{1,0:T(2,128)} %bitcast.9, f32[512,128]{1,0:T(8,128)} %bitcast.6, f32[512,128]{1,0:T(8,128)} %bitcast.7), custom_call_target="tpu_custom_call" | custom-call | tf_op jit(solution)/shard_map/pallas_call | solution.py:784
  103.0 0.0 copy-start
  103.0 1.7 %copy.13 = f32[65536]{0:T(1024)} copy(f32[65536]{0:T(1024)} %bitcast.8) | data formatting | bytes 524288
  105.3 0.0 copy-done
  105.3 0.6 copy.15
Async XLA Ops:
  103.0 2.4 %copy-start = (f32[25,25]{1,0:T(8,128)S(1)}, f32[25,25]{1,0:T(8,128)}, u32[]{:S(2)}) copy-start(f32[25,25]{1,0:T(8,128)} %get-tuple-element.18) | copy-start | bytes 7504

commit v4 on v3

--- a/solution.py
+++ b/solution.py
@@ -20,8 +20,7 @@
 FIRST_DEVICE_BIT = 16
 CROSS = ((16, "grp", 1), (17, "grp", 2), (18, "grp", 4), (19, "grp", 8), (24, "wide", 16))
 STAGES = (
-    (((1,), ()),),
-    (((2,), ()), ((), (16,)), ((2,), (16,))),
+    (((1,), ()), ((2,), ()), ((1, 2), ()), ((), (16,)), ((1,), (16,)), ((2,), (16,)), ((1, 2), (16,))),
     (((4,), ()), ((8,), ()), ((4, 8), ())),
     tuple(((), tuple(2**bit for bit in range(4) if mask >> bit & 1)) for mask in range(1, 16)),
 )
@@ -531,7 +530,7 @@
     ]
     done = 0
     for number, service in enumerate(services):
-        goal = max(6, len(tasks) * (number + 1) // (len(services) + 1))
+        goal = 6 + 2 * number
         while done < goal:
             tasks[done]()
             done += 1
@@ -722,8 +721,7 @@
     tasks += [collect(tuple(range(16)) + (20, 25, 26))]
     tasks += [gradient_cross(number) for number in range(len(CROSS))]
     tasks += [collect((16, 17, 18, 19, 24))]
-    for bit in (1, 2, 3):
-        tasks += [gradient_ring(bit), collect((20 + bit,))]
+    tasks += [gradient_ring(1), gradient_ring(2), collect((21, 22)), gradient_ring(3), collect((23,))]
     for task in tasks:
         task()
 

time: 109 us -> 108 us (level)
  no operation moved by 1% of the time
where the time goes in v4:
time: 108 us
  Pallas kernels  102 us (94%)
  between operations  4.3 us (4%)
  local copies, waits for them, and re-layouts  2.29 us (2%)
    pallas_call x1, Pallas kernels, body(): pl.pallas_call(kernel, out_shape=(jax.ShapeDtypeStruct((ROWS, LANES), F32...  102 us
    unnamed x4, local copies, waits for them, and re-layouts  2.29 us

profile of v4, /device:TPU:1, one launch (start us, length us, event | category | flops | bytes accessed | tf_op | source)
XLA Modules:
  0.0 108.2 jit_solution(1476776109529114393)
XLA Ops:
  0.6 101.6 %shard_map.84 = (f32[512,128]{1,0:T(8,128)}, f32[25,25]{1,0:T(8,128)}, f32[1,1]{1,0:T(1,128)}, f32[1,1]{1,0:T(1,128)}) custom-call(f32[25,25]{1,0:T(8,128)} %hazards_hbm.1, s32[25]{0:T(128)} %order_hbm.1, s32[2,128]{1,0:T(2,128)} %bitcast.9, f32[512,128]{1,0:T(8,128)} %bitcast.6, f32[512,128]{1,0:T(8,128)} %bitcast.7), custom_call_target="tpu_custom_call" | custom-call | tf_op jit(solution)/shard_map/pallas_call | solution.py:782
  102.2 0.0 copy-start
  102.3 1.7 %copy.13 = f32[65536]{0:T(1024)} copy(f32[65536]{0:T(1024)} %bitcast.8) | data formatting | bytes 524288
  104.6 0.0 copy-done
  104.6 0.6 copy.15
Async XLA Ops:
  102.2 2.4 %copy-start = (f32[25,25]{1,0:T(8,128)S(1)}, f32[25,25]{1,0:T(8,128)}, u32[]{:S(2)}) copy-start(f32[25,25]{1,0:T(8,128)} %get-tuple-element.18) | copy-start | bytes 7504
